TPU v7x, 32 devices: a whole 2x2x4 slice. The times are simulated.
32 devices in a mesh: dp: 4 (over z), row: 2 (over x), col: 4 (over y, core).
Axes of the slice: x: 2, y: 2, z: 4, core: 2. Of those that a mesh axis runs over, the one named last changes fastest.
Arguments:
- tokens: bfloat16 [768, 16384], P(('row', 'col'), 'dp'), may hold values from -6 to 6
- cotangent: bfloat16 [768, 16384], P(('row', 'col'), 'dp'), may hold values from -6 to 6
- holder_of: int32 [8, 4], replicated, may hold values from 0 to 3, each once within a row
- lengths: int32 [8, 4, 4], replicated, may hold values from 0 to 512, as said below
- input_gain: float32 [768], P(('row', 'col')), may hold values from 0.5 to 1.5
- input_shift: float32 [768], P(('row', 'col')), may hold values from -1.5 to 1.5
- attend_weight: bfloat16 [3, 768, 768], P(None, 'col', 'row'), may hold values from -0.21875 to 0.21875
- attend_bias: float32 [2, 768], P(None, 'col'), may hold values from -1.5 to 1.5
- mixed_gain: float32 [768], P('col'), may hold values from 0.5 to 1.5
- mixed_shift: float32 [768], P('col'), may hold values from -1.5 to 1.5
- output_weight: bfloat16 [768, 768], P('col', 'row'), may hold values from -0.375 to 0.375
- output_bias: float32 [768], P(('row', 'col')), may hold values from -1.5 to 1.5
- middle_gain: float32 [768], P(('row', 'col')), may hold values from 0.5 to 1.5
- middle_shift: float32 [768], P(('row', 'col')), may hold values from -1.5 to 1.5
- expand_weight: bfloat16 [768, 3072], P('row', 'col'), may hold values from -0.375 to 0.375
- expand_bias: float32 [3072], P('col'), may hold values from -1.5 to 1.5
- hidden_gain: float32 [3072], P('col'), may hold values from 0.5 to 1.5
- hidden_shift: float32 [3072], P('col'), may hold values from -1.5 to 1.5
- shrink_weight: bfloat16 [3072, 768], P('col', 'row'), may hold values from -0.1875 to 0.1875
- shrink_bias: float32 [768], P(('row', 'col')), may hold values from -1.5 to 1.5
Outputs:
- block_out: bfloat16 [768, 16384], P(('row', 'col'), 'dp')
- input_grad: bfloat16 [768, 16384], P(('row', 'col'), 'dp')
- input_gain_grad: float32 [768], P(('row', 'col'))
- input_shift_grad: float32 [768], P(('row', 'col'))
- attend_weight_grad: float32 [3, 768, 768], P(None, 'col', 'row')
- attend_bias_grad: float32 [2, 768], P(None, 'col')
- mixed_gain_grad: float32 [768], P('col')
- mixed_shift_grad: float32 [768], P('col')
- output_weight_grad: float32 [768, 768], P('col', 'row')
- output_bias_grad: float32 [768], P(('row', 'col'))
- middle_gain_grad: float32 [768], P(('row', 'col'))
- middle_shift_grad: float32 [768], P(('row', 'col'))
- expand_weight_grad: float32 [768, 3072], P('row', 'col')
- expand_bias_grad: float32 [3072], P('col')
- hidden_gain_grad: float32 [3072], P('col')
- hidden_shift_grad: float32 [3072], P('col')
- shrink_weight_grad: float32 [3072, 768], P('col', 'row')
- shrink_bias_grad: float32 [768], P(('row', 'col'))
Inputs may be any that keep to these rules, and one draw needn't show every extreme that they name: Each row of holder_of names every holder once. The 4 lengths of a unit add up to 512; a zero length is an empty slot; in every micro-batch one unit is a single sequence of 512 tokens.
All inputs are finite; a program needn't handle non-finite values.
Results may differ from a plain program's by a relative error of at most 0.017.
Values may be sent and summed in bfloat16 or wider, within the bound.
No kernel may reach another device: no remote copies, remote signals or barrier semaphores. Data moves between devices by JAX's collectives and lax.ppermute only.
A program may use at most 128 MiB of HBM per device.

v0:
```python
import math

import jax
import jax.numpy as jnp
from jax import lax
from jax.sharding import PartitionSpec as P

D = 768
HEAD = 64
FF = 3072


norm_eps = 1e-05
masked_score = -1e30


def wide_sums(partials):
    return lax.psum(partials, ("row", "col"))


def narrow_sums(partials):
    return lax.psum(partials, "col")


def feature_gather(values):
    return lax.all_gather(values, "col", axis=1, tiled=True)


def token_scatter(values):
    return lax.psum_scatter(values, "row", scatter_dimension=0, tiled=True)


def token_gather(values):
    return lax.all_gather(values, "row", axis=0, tiled=True)


def feature_scatter(values):
    return lax.psum_scatter(values, "col", scatter_dimension=1, tiled=True)


def gelu_exact(values):
    return jax.nn.gelu(values, approximate=False)


def normalize(values, gain_vec, offset, feature_count, reducer):
    row_sums = reducer((jnp.sum(values, axis=1), jnp.sum(values * values, axis=1)))
    center = row_sums[0] / feature_count
    spread = lax.rsqrt(row_sums[1] / feature_count - center * center + norm_eps)
    normed = (values - center[:, None]) * spread[:, None]
    return (normed * gain_vec + offset, center, spread)


def normalize_back(upward, values, center, spread, gain_vec, feature_count, reducer):
    normed = (values - center[:, None]) * spread[:, None]
    scaled = upward * gain_vec
    row_sums = reducer((jnp.sum(scaled, axis=1), jnp.sum(scaled * normed, axis=1)))
    inward = (
        scaled
        - (row_sums[0] / feature_count)[:, None]
        - normed * (row_sums[1] / feature_count)[:, None]
    ) * spread[:, None]
    return (inward, jnp.sum(upward * normed, axis=0), jnp.sum(upward, axis=0))


def split_heads(values):
    return values.reshape(values.shape[0], values.shape[1] // HEAD, HEAD)


def attend_scores(queries, keys_all, query_seg, key_seg):
    scores = jnp.einsum(
        "qhe,khe->hqk",
        split_heads(queries),
        split_heads(keys_all),
        preferred_element_type=jnp.float32,
    ) * (1.0 / math.sqrt(HEAD))
    visible = query_seg[:, None] == key_seg[None, :]
    return jnp.where(visible[None], scores, masked_score)


def attend_forward(queries, keys_all, values_all, query_seg, key_seg):
    scores = attend_scores(queries, keys_all, query_seg, key_seg)
    top_score = jnp.max(scores, axis=2, keepdims=True)
    raised = jnp.exp(scores - top_score)
    denominator = jnp.sum(raised, axis=2, keepdims=True)
    probability = (raised / denominator).astype(jnp.bfloat16)
    mixed = jnp.einsum(
        "hqk,khe->qhe", probability, split_heads(values_all), preferred_element_type=jnp.float32
    )
    return (mixed.reshape(queries.shape[0], queries.shape[1]), top_score + jnp.log(denominator))


def attend_backward(grad_mixed, queries, keys_all, values_all, log_total, query_seg, key_seg):
    probability = jnp.exp(attend_scores(queries, keys_all, query_seg, key_seg) - log_total)
    grad_heads = split_heads(grad_mixed)
    grad_prob = jnp.einsum(
        "qhe,khe->hqk", grad_heads, split_heads(values_all), preferred_element_type=jnp.float32
    )
    inner_sum = jnp.sum(probability * grad_prob, axis=2, keepdims=True)
    grad_scores = (probability * (grad_prob - inner_sum)).astype(jnp.bfloat16)
    score_scale = 1.0 / math.sqrt(HEAD)
    grad_query = (
        jnp.einsum(
            "hqk,khe->qhe", grad_scores, split_heads(keys_all), preferred_element_type=jnp.float32
        )
        * score_scale
    )
    grad_key = (
        jnp.einsum(
            "hqk,qhe->khe", grad_scores, split_heads(queries), preferred_element_type=jnp.float32
        )
        * score_scale
    )
    grad_value = jnp.einsum(
        "hqk,qhe->khe",
        probability.astype(jnp.bfloat16),
        grad_heads,
        preferred_element_type=jnp.float32,
    )
    width_all = queries.shape[1]
    return (
        grad_query.reshape(-1, width_all),
        grad_key.reshape(-1, width_all),
        grad_value.reshape(-1, width_all),
    )


def first_forward(full_in, local_weight):
    summed = token_scatter(jnp.dot(full_in, local_weight, preferred_element_type=jnp.float32))
    return (summed, full_in)


def first_backward(grad_half, stored, local_weight):
    grad_full = token_gather(grad_half)
    weight_step = jnp.einsum("tk,tn->kn", stored, grad_full, preferred_element_type=jnp.float32)
    partial_in = jnp.einsum(
        "tn,kn->tk", grad_full, local_weight, preferred_element_type=jnp.float32
    )
    return (feature_scatter(partial_in), weight_step)


def body(
    tokens,
    cotangent,
    holder_of,
    lengths,
    input_gain,
    input_shift,
    attend_weight,
    attend_bias,
    mixed_gain,
    mixed_shift,
    output_weight,
    output_bias,
    middle_gain,
    middle_shift,
    expand_weight,
    expand_bias,
    hidden_gain,
    hidden_shift,
    shrink_weight,
    shrink_bias,
):
    holders = lax.axis_size("dp")
    half_count = holders // 2
    holder = lax.axis_index("dp")
    row_pos = lax.axis_index("row")
    row_count = lax.axis_size("row")
    micro_count = holder_of.shape[0]
    feature_local = tokens.shape[0]
    block_rows = tokens.shape[1] // (micro_count * half_count)
    unit_rows = half_count * block_rows
    query_rows = unit_rows // row_count
    half_side = holder // half_count
    paired = holder_of.reshape(micro_count, half_count, 2)
    target = lax.dynamic_index_in_dim(paired, half_side, axis=2, keepdims=False)
    routing = (target[:, None, :] == jnp.arange(holders, dtype=jnp.int32)[None, :, None]).astype(
        jnp.bfloat16
    )

    def outgoing(stacked):
        blocks = stacked.reshape(feature_local, micro_count, half_count, block_rows)
        return jnp.einsum(
            "meb,wmbt->metw", routing, blocks, preferred_element_type=jnp.float32
        ).astype(jnp.bfloat16)

    arrived_in, arrived_cot = (
        lax.all_to_all(outgoing(tokens), "dp", split_axis=1, concat_axis=1, tiled=True),
        lax.all_to_all(outgoing(cotangent), "dp", split_axis=1, concat_axis=1, tiled=True),
    )
    owned = (holder_of == holder).astype(jnp.int32)
    unit_id = jnp.sum(owned * jnp.arange(holders, dtype=jnp.int32)[None, :], axis=1)
    first_source = unit_id % 2 * half_count

    def take_sources(received, start_at):
        return lax.dynamic_slice_in_dim(received, start_at, half_count, 0)

    def pick(arrived):
        chosen = jax.vmap(take_sources)(arrived, first_source)
        return chosen.reshape(micro_count, unit_rows, feature_local)

    in_units = pick(arrived_in)
    cot_units = pick(arrived_cot)
    unit_lengths = lax.dynamic_index_in_dim(lengths, holder, axis=1, keepdims=False)
    bounds = jnp.cumsum(unit_lengths, axis=1)[:, :-1]
    positions = jnp.arange(unit_rows, dtype=jnp.int32)
    segments = jnp.sum((positions[None, :, None] >= bounds[:, None, :]).astype(jnp.int32), axis=2)
    attend_rows = attend_weight.shape[2]
    head_width = attend_weight.shape[1]
    attend_local = jnp.transpose(attend_weight, (2, 0, 1)).reshape(attend_rows, 3 * head_width)

    def forward_step(carried, inputs):
        unit_in, segment = inputs
        residual = unit_in.astype(jnp.float32)
        query_seg = lax.dynamic_slice_in_dim(segment, row_pos * query_rows, query_rows, 0)
        normed_in, center_in, spread_in = normalize(residual, input_gain, input_shift, D, wide_sums)
        gathered_in = feature_gather(normed_in.astype(jnp.bfloat16))
        triple, stored_first = first_forward(gathered_in, attend_local)
        triple = triple.reshape(triple.shape[0], 3, head_width)
        queries = (triple[:, 0] + attend_bias[0]).astype(jnp.bfloat16)
        keys_half = triple[:, 1].astype(jnp.bfloat16)
        values_half = (triple[:, 2] + attend_bias[1]).astype(jnp.bfloat16)
        key_value = token_gather(jnp.concatenate([keys_half, values_half], axis=1))
        mixed, log_total = attend_forward(
            queries, key_value[:, :head_width], key_value[:, head_width:], query_seg, segment
        )
        mixed_norm, center_mix, spread_mix = normalize(
            mixed, mixed_gain, mixed_shift, D, narrow_sums
        )
        mixed_all = token_gather(mixed_norm.astype(jnp.bfloat16))
        attend_part = feature_scatter(
            jnp.dot(mixed_all, output_weight, preferred_element_type=jnp.float32)
        )
        middle = residual + attend_part + output_bias
        middle_norm, center_mid, spread_mid = normalize(
            middle, middle_gain, middle_shift, D, wide_sums
        )
        middle_all = feature_gather(middle_norm.astype(jnp.bfloat16))
        expanded, stored_second = first_forward(middle_all, expand_weight)
        expanded = expanded + expand_bias
        hidden_norm, center_hid, spread_hid = normalize(
            gelu_exact(expanded), hidden_gain, hidden_shift, FF, narrow_sums
        )
        hidden_all = token_gather(hidden_norm.astype(jnp.bfloat16))
        shrunk = feature_scatter(
            jnp.dot(hidden_all, shrink_weight, preferred_element_type=jnp.float32)
        )
        result = (middle + shrunk + shrink_bias).astype(jnp.bfloat16)
        stored = (
            center_in,
            spread_in,
            stored_first,
            queries,
            key_value,
            log_total,
            mixed,
            center_mix,
            spread_mix,
            mixed_all,
            middle,
            center_mid,
            spread_mid,
            stored_second,
            expanded,
            center_hid,
            spread_hid,
            hidden_all,
        )
        return (carried, (result, stored))

    _, (out_units, stored_all) = lax.scan(
        forward_step, jnp.zeros((), jnp.float32), (in_units, segments)
    )

    def zeros_like_f32(values):
        return jnp.zeros(values.shape, jnp.float32)

    totals_init = (
        zeros_like_f32(input_gain),
        zeros_like_f32(input_shift),
        zeros_like_f32(attend_local),
        zeros_like_f32(attend_bias),
        zeros_like_f32(mixed_gain),
        zeros_like_f32(mixed_shift),
        zeros_like_f32(output_weight),
        zeros_like_f32(output_bias),
        zeros_like_f32(middle_gain),
        zeros_like_f32(middle_shift),
        zeros_like_f32(expand_weight),
        zeros_like_f32(expand_bias),
        zeros_like_f32(hidden_gain),
        zeros_like_f32(hidden_shift),
        zeros_like_f32(shrink_weight),
        zeros_like_f32(shrink_bias),
    )

    def backward_step(totals, inputs):
        cot_unit, segment, unit_in, stored = inputs
        (
            center_in,
            spread_in,
            stored_first,
            queries,
            key_value,
            log_total,
            mixed,
            center_mix,
            spread_mix,
            mixed_all,
            middle,
            center_mid,
            spread_mid,
            stored_second,
            expanded,
            center_hid,
            spread_hid,
            hidden_all,
        ) = stored
        query_seg = lax.dynamic_slice_in_dim(segment, row_pos * query_rows, query_rows, 0)
        upstream = cot_unit.astype(jnp.float32)
        shrink_local = upstream.astype(jnp.bfloat16)
        step_shrink_b = jnp.sum(shrink_local.astype(jnp.float32), axis=0)
        shrink_all = feature_gather(shrink_local)
        step_shrink_w = jnp.einsum(
            "tf,td->fd", hidden_all, shrink_all, preferred_element_type=jnp.float32
        )
        grad_hidden = token_scatter(
            jnp.einsum("td,fd->tf", shrink_all, shrink_weight, preferred_element_type=jnp.float32)
        )
        activated, gelu_pull = jax.vjp(gelu_exact, expanded)
        grad_act, step_hid_g, step_hid_s = normalize_back(
            grad_hidden, activated, center_hid, spread_hid, hidden_gain, FF, narrow_sums
        )
        grad_expand = gelu_pull(grad_act)[0].astype(jnp.bfloat16)
        step_exp_b = jnp.sum(grad_expand.astype(jnp.float32), axis=0)
        grad_mid_norm, step_exp_w = first_backward(grad_expand, stored_second, expand_weight)
        grad_mid_in, step_mid_g, step_mid_s = normalize_back(
            grad_mid_norm, middle, center_mid, spread_mid, middle_gain, D, wide_sums
        )
        grad_middle = upstream + grad_mid_in
        attend_local_grad = grad_middle.astype(jnp.bfloat16)
        step_out_b = jnp.sum(attend_local_grad.astype(jnp.float32), axis=0)
        attend_all = feature_gather(attend_local_grad)
        step_out_w = jnp.einsum(
            "th,td->hd", mixed_all, attend_all, preferred_element_type=jnp.float32
        )
        grad_mix_norm = token_scatter(
            jnp.einsum("td,hd->th", attend_all, output_weight, preferred_element_type=jnp.float32)
        )
        grad_mixed, step_mix_g, step_mix_s = normalize_back(
            grad_mix_norm, mixed, center_mix, spread_mix, mixed_gain, D, narrow_sums
        )
        grad_query, grad_key, grad_value = attend_backward(
            grad_mixed.astype(jnp.bfloat16),
            queries,
            key_value[:, :head_width],
            key_value[:, head_width:],
            log_total,
            query_seg,
            segment,
        )
        key_value_grad = token_scatter(jnp.concatenate([grad_key, grad_value], axis=1)).astype(
            jnp.bfloat16
        )
        query_grad = grad_query.astype(jnp.bfloat16)
        step_att_b = jnp.stack(
            [
                jnp.sum(query_grad.astype(jnp.float32), axis=0),
                jnp.sum(key_value_grad[:, head_width:].astype(jnp.float32), axis=0),
            ]
        )
        grad_triple = jnp.concatenate([query_grad, key_value_grad], axis=1)
        grad_in_norm, step_att_w = first_backward(grad_triple, stored_first, attend_local)
        grad_in_part, step_in_g, step_in_s = normalize_back(
            grad_in_norm,
            unit_in.astype(jnp.float32),
            center_in,
            spread_in,
            input_gain,
            D,
            wide_sums,
        )
        grad_unit = grad_middle + grad_in_part
        steps_all = (
            step_in_g,
            step_in_s,
            step_att_w,
            step_att_b,
            step_mix_g,
            step_mix_s,
            step_out_w,
            step_out_b,
            step_mid_g,
            step_mid_s,
            step_exp_w,
            step_exp_b,
            step_hid_g,
            step_hid_s,
            step_shrink_w,
            step_shrink_b,
        )
        totals = tuple((running + added for running, added in zip(totals, steps_all)))
        return (totals, grad_unit.astype(jnp.bfloat16))

    totals, grad_units = lax.scan(
        backward_step, totals_init, (cot_units, segments, in_units, stored_all), reverse=True
    )
    attend_sum = totals[2]
    expand_sum = totals[10]
    (
        in_gain_g,
        in_shift_g,
        attend_w_g,
        out_w_g,
        out_b_g,
        mid_gain_g,
        mid_shift_g,
        expand_w_g,
        shrink_w_g,
        shrink_b_g,
    ) = (
        lax.psum(totals[0].astype(jnp.bfloat16), "dp").astype(jnp.float32),
        lax.psum(totals[1].astype(jnp.bfloat16), "dp").astype(jnp.float32),
        lax.psum(attend_sum.astype(jnp.bfloat16), "dp").astype(jnp.float32),
        lax.psum(totals[6].astype(jnp.bfloat16), "dp").astype(jnp.float32),
        lax.psum(totals[7].astype(jnp.bfloat16), "dp").astype(jnp.float32),
        lax.psum(totals[8].astype(jnp.bfloat16), "dp").astype(jnp.float32),
        lax.psum(totals[9].astype(jnp.bfloat16), "dp").astype(jnp.float32),
        lax.psum(expand_sum.astype(jnp.bfloat16), "dp").astype(jnp.float32),
        lax.psum(totals[14].astype(jnp.bfloat16), "dp").astype(jnp.float32),
        lax.psum(totals[15].astype(jnp.bfloat16), "dp").astype(jnp.float32),
    )
    attend_b_g, mix_gain_g, mix_shift_g, expand_b_g, hid_gain_g, hid_shift_g = lax.psum(
        (totals[3], totals[4], totals[5], totals[11], totals[12], totals[13]), ("dp", "row")
    )

    def place_piece(block_piece, start_at):
        blank = jnp.zeros((holders, block_rows, feature_local), jnp.bfloat16)
        return lax.dynamic_update_slice_in_dim(blank, block_piece, start_at, 0)

    def send_back(units):
        pieces = units.reshape(micro_count, half_count, block_rows, feature_local)
        return jax.vmap(place_piece)(pieces, first_source)

    back_out, back_grad = (
        lax.all_to_all(send_back(out_units), "dp", split_axis=1, concat_axis=1, tiled=True),
        lax.all_to_all(send_back(grad_units), "dp", split_axis=1, concat_axis=1, tiled=True),
    )

    def restore(arrived):
        ordered = jnp.einsum("meb,metw->wmbt", routing, arrived, preferred_element_type=jnp.float32)
        return ordered.reshape(tokens.shape).astype(jnp.bfloat16)

    attend_w_out = jnp.transpose(attend_w_g.reshape(attend_rows, 3, head_width), (1, 2, 0))
    return (
        restore(back_out),
        restore(back_grad),
        in_gain_g,
        in_shift_g,
        attend_w_out,
        attend_b_g,
        mix_gain_g,
        mix_shift_g,
        out_w_g,
        out_b_g,
        mid_gain_g,
        mid_shift_g,
        expand_w_g,
        expand_b_g,
        hid_gain_g,
        hid_shift_g,
        shrink_w_g,
        shrink_b_g,
    )


def solution(mesh):
    in_specs = (
        P(("row", "col"), "dp"),
        P(("row", "col"), "dp"),
        P(),
        P(),
        P(("row", "col")),
        P(("row", "col")),
        P(None, "col", "row"),
        P(None, "col"),
        P("col"),
        P("col"),
        P("col", "row"),
        P(("row", "col")),
        P(("row", "col")),
        P(("row", "col")),
        P("row", "col"),
        P("col"),
        P("col"),
        P("col"),
        P("col", "row"),
        P(("row", "col")),
    )
    out_specs = (
        P(("row", "col"), "dp"),
        P(("row", "col"), "dp"),
        P(("row", "col")),
        P(("row", "col")),
        P(None, "col", "row"),
        P(None, "col"),
        P("col"),
        P("col"),
        P("col", "row"),
        P(("row", "col")),
        P(("row", "col")),
        P(("row", "col")),
        P("row", "col"),
        P("col"),
        P("col"),
        P("col"),
        P("col", "row"),
        P(("row", "col")),
    )
    return jax.shard_map(body, mesh=mesh, in_specs=in_specs, out_specs=out_specs, check_vma=False)
```

profile of v0, /device:TPU:0, one launch (start us, length us, event | category | flops | bytes accessed | tf_op | source)
XLA Modules:
  0.0 3525.9 jit_solution(14907036112206222545)
XLA Ops:
  24.4 33.4 all-to-all-done
  65.4 33.3 all-to-all-done.2
  102.8 1522.9 %while.99 = (s32[]{:T(128)}, bf16[8,512,96]{1,2,0:T(8,128)(2,1)}, f32[8,512]{1,0:T(8,128)}, f32[8,512]{1,0:T(8,128)}, bf16[8,512,384]{1,2,0:T(8,128)(2,1)}, /*in...) while((s32[]{:T(128)}, bf16[8,512,96]{1,2,0:T(8,128)(2,1)}, ...), condition=%wide.region_26.27_spmd, body=%wide.region_3.26_spmd.sunk | while | flops 1026775808 | bytes 52225956 | solution.py:270
  170.8 23.6 reduce-scatter.12.cloned.1.call-done
  315.3 20.9 reduce-scatter.10.cloned.1.call-done
  361.4 23.6 reduce-scatter.12.cloned.1.call-done
  505.9 21.0 reduce-scatter.10.cloned.1.call-done
  552.0 23.6 reduce-scatter.12.cloned.1.call-done
  696.5 20.9 reduce-scatter.10.cloned.1.call-done
  742.6 23.6 reduce-scatter.12.cloned.1.call-done
  887.1 20.9 reduce-scatter.10.cloned.1.call-done
  933.2 23.6 reduce-scatter.12.cloned.1.call-done
  1077.7 20.9 reduce-scatter.10.cloned.1.call-done
  1123.8 23.6 reduce-scatter.12.cloned.1.call-done
  1268.3 20.9 reduce-scatter.10.cloned.1.call-done
  1314.3 23.6 reduce-scatter.12.cloned.1.call-done
  1458.8 20.9 reduce-scatter.10.cloned.1.call-done
  1504.9 23.6 reduce-scatter.12.cloned.1.call-done
  1626.7 1615.2 %while.102 = (s32[]{:T(128)}, f32[96]{0:T(128)}, f32[96]{0:T(128)}, f32[384,576]{0,1:T(8,128)}, f32[2,192]{1,0:T(2,128)}, /*index=5*/f32[192]{0:T(256)}, f32[192...) while((s32[]{:T(128)}, f32[96]{0:T(128)}, f32[96]{0:T(128)}, ...), condition=%wide.region_64.65_spmd.clone, body=%wide.region_28.64_spmd.clone.sunk | while | flops 2092783872 | bytes 73503512 | solution.py:404
  1638.1 25.8 reduce-scatter.18.cloned.1.call-done
  1840.8 24.9 reduce-scatter.18.cloned.1.call-done
  2042.6 24.9 reduce-scatter.18.cloned.1.call-done
  2244.4 24.9 reduce-scatter.18.cloned.1.call-done
  2446.1 24.9 reduce-scatter.18.cloned.1.call-done
  2647.9 24.9 reduce-scatter.18.cloned.1.call-done
  2701.1 20.1 reduce-scatter.20.cloned.1.call-done
  2849.8 24.9 reduce-scatter.18.cloned.1.call-done
  3051.5 24.9 reduce-scatter.18.cloned.1.call-done
  3244.9 71.3 %while.101 = (s32[]{:T(128)}, bf16[8,4,256,96]{2,3,0,1:T(8,128)(2,1)}, s32[8,4]{0,1:T(4,128)S(1)}, bf16[8,2,256,96]{3,2,1,0:T(8,128)(2,1)S(1)}, s32[]{:T(128)}, /*index=5*/s32[4]{0:T(128)S(1)}) while((s32[]{:T(128)}, bf16[8,4,256,96]{2,3,0,1:T(8,128)(2,1)}, s32[8,4]{0,1:T(4,128)S(1)}, bf16[8,2,256,96]{3,2,1,0:T(8,128)(2,1)S(1)}, s32[]{:T(128)}, ...), condition=%wide.while_cond.1, body=%wide.while_body.1.sunk | while | flops 49181 | bytes 1082551 | solution.py:438
  3322.9 71.6 %while.100 = (s32[]{:T(128)}, bf16[8,4,256,96]{2,3,0,1:T(8,128)(2,1)}, s32[8,4]{0,1:T(4,128)S(1)}, bf16[8,2,256,96]{3,2,1,0:T(8,128)(2,1)S(1)}, s32[]{:T(128)}, /*index=5*/s32[4]{0:T(128)S(1)}) while((s32[]{:T(128)}, bf16[8,4,256,96]{2,3,0,1:T(8,128)(2,1)}, s32[8,4]{0,1:T(4,128)S(1)}, bf16[8,2,256,96]{3,2,1,0:T(8,128)(2,1)S(1)}, s32[]{:T(128)}, ...), condition=%wide.while_cond, body=%wide.while_body.sunk | while | flops 49181 | bytes 1082551 | solution.py:438
  3404.9 43.7 %all-reduce.10 = (bf16[96]{0:T(256)(128)(2,1)S(1)}, bf16[96]{0:T(256)(128)(2,1)S(1)}, bf16[96]{0:T(256)(128)(2,1)S(1)}, bf16[96]{0:T(256)(128)(2,1)S(1)}, bf16[9...) all-reduce(bf16[96]{0:T(256)(128)(2,1)S(1)} %convert_element_type.3, ...), channel_id=1, replica_groups=mesh['dp'=4,'row'=2,'col'=4] {'dp'}, use_global_device_ids=true, to_apply=%region_66.67 | all-reduce | flops 576 | bytes 2304 | tf_op jit(solution)/shard_map/psum | solution.py:421
  3451.7 53.8 %all-reduce.9 = (f32[2,192]{1,0:T(2,128)}, f32[192]{0:T(256)}, f32[192]{0:T(256)}, f32[768]{0:T(1024)}, f32[768]{0:T(1024)}, /*index=5*/f32[768]{0:T(1024)}) all-reduce(f32[2,192]{1,0:T(2,128)S(1)} %copy-done.46, f32[192]{0:T(256)S(1)} %copy-done.55, f32[192]{0:T(256)S(1)} %copy-done.58, ...), channel_id=1, replica_groups=mesh['dp'=4,'row'=2,'col'=4] {'dp','row'}, use_global_device_ids=true, to_apply=%region_69.70 | all-reduce | flops 3072 | bytes 24576 | tf_op jit(solution)/shard_map/psum | solution.py:432
  (2176 shorter events, 2783.0 us)
Async XLA Ops:
  170.8 72.9 %reduce-scatter.14.cloned.1.call-start = ((), (), s32[]{:S(2)}) async-start(), calls=%async_computation.16 | async-start | bytes 2359296 | tf_op jit(solution)/shard_map/while/body/eval_jaxpr/reduce_scatter | solution.py:30
  218.0 72.0 %reduce-scatter.16.cloned.1.call-start = ((), (), s32[]{:S(2)}) async-start(), calls=%async_computation.17 | async-start | bytes 983040 | tf_op jit(solution)/shard_map/while/body/eval_jaxpr/reduce_scatter | solution.py:38
  314.9 70.1 %reduce-scatter.12.cloned.1.call-start = ((), (), s32[]{:S(2)}) async-start(), calls=%async_computation.15 | async-start | bytes 983040 | tf_op jit(solution)/shard_map/while/body/eval_jaxpr/reduce_scatter | solution.py:38
  361.4 72.9 %reduce-scatter.14.cloned.1.call-start = ((), (), s32[]{:S(2)}) async-start(), calls=%async_computation.16 | async-start | bytes 2359296 | tf_op jit(solution)/shard_map/while/body/eval_jaxpr/reduce_scatter | solution.py:30
  408.6 72.0 %reduce-scatter.16.cloned.1.call-start = ((), (), s32[]{:S(2)}) async-start(), calls=%async_computation.17 | async-start | bytes 983040 | tf_op jit(solution)/shard_map/while/body/eval_jaxpr/reduce_scatter | solution.py:38
  505.5 70.1 %reduce-scatter.12.cloned.1.call-start = ((), (), s32[]{:S(2)}) async-start(), calls=%async_computation.15 | async-start | bytes 983040 | tf_op jit(solution)/shard_map/while/body/eval_jaxpr/reduce_scatter | solution.py:38
  552.0 72.9 %reduce-scatter.14.cloned.1.call-start = ((), (), s32[]{:S(2)}) async-start(), calls=%async_computation.16 | async-start | bytes 2359296 | tf_op jit(solution)/shard_map/while/body/eval_jaxpr/reduce_scatter | solution.py:30
  599.2 72.0 %reduce-scatter.16.cloned.1.call-start = ((), (), s32[]{:S(2)}) async-start(), calls=%async_computation.17 | async-start | bytes 983040 | tf_op jit(solution)/shard_map/while/body/eval_jaxpr/reduce_scatter | solution.py:38
  696.1 70.1 %reduce-scatter.12.cloned.1.call-start = ((), (), s32[]{:S(2)}) async-start(), calls=%async_computation.15 | async-start | bytes 983040 | tf_op jit(solution)/shard_map/while/body/eval_jaxpr/reduce_scatter | solution.py:38
  742.5 72.9 %reduce-scatter.14.cloned.1.call-start = ((), (), s32[]{:S(2)}) async-start(), calls=%async_computation.16 | async-start | bytes 2359296 | tf_op jit(solution)/shard_map/while/body/eval_jaxpr/reduce_scatter | solution.py:30
  789.8 72.0 %reduce-scatter.16.cloned.1.call-start = ((), (), s32[]{:S(2)}) async-start(), calls=%async_computation.17 | async-start | bytes 983040 | tf_op jit(solution)/shard_map/while/body/eval_jaxpr/reduce_scatter | solution.py:38
  933.1 72.9 %reduce-scatter.14.cloned.1.call-start = ((), (), s32[]{:S(2)}) async-start(), calls=%async_computation.16 | async-start | bytes 2359296 | tf_op jit(solution)/shard_map/while/body/eval_jaxpr/reduce_scatter | solution.py:30
  980.3 72.0 %reduce-scatter.16.cloned.1.call-start = ((), (), s32[]{:S(2)}) async-start(), calls=%async_computation.17 | async-start | bytes 983040 | tf_op jit(solution)/shard_map/while/body/eval_jaxpr/reduce_scatter | solution.py:38
  1123.7 72.9 %reduce-scatter.14.cloned.1.call-start = ((), (), s32[]{:S(2)}) async-start(), calls=%async_computation.16 | async-start | bytes 2359296 | tf_op jit(solution)/shard_map/while/body/eval_jaxpr/reduce_scatter | solution.py:30
  1170.9 72.0 %reduce-scatter.16.cloned.1.call-start = ((), (), s32[]{:S(2)}) async-start(), calls=%async_computation.17 | async-start | bytes 983040 | tf_op jit(solution)/shard_map/while/body/eval_jaxpr/reduce_scatter | solution.py:38
  1267.9 70.1 %reduce-scatter.12.cloned.1.call-start = ((), (), s32[]{:S(2)}) async-start(), calls=%async_computation.15 | async-start | bytes 983040 | tf_op jit(solution)/shard_map/while/body/eval_jaxpr/reduce_scatter | solution.py:38
  1314.3 72.9 %reduce-scatter.14.cloned.1.call-start = ((), (), s32[]{:S(2)}) async-start(), calls=%async_computation.16 | async-start | bytes 2359296 | tf_op jit(solution)/shard_map/while/body/eval_jaxpr/reduce_scatter | solution.py:30
  1361.5 72.0 %reduce-scatter.16.cloned.1.call-start = ((), (), s32[]{:S(2)}) async-start(), calls=%async_computation.17 | async-start | bytes 983040 | tf_op jit(solution)/shard_map/while/body/eval_jaxpr/reduce_scatter | solution.py:38
  1458.4 70.1 %reduce-scatter.12.cloned.1.call-start = ((), (), s32[]{:S(2)}) async-start(), calls=%async_computation.15 | async-start | bytes 983040 | tf_op jit(solution)/shard_map/while/body/eval_jaxpr/reduce_scatter | solution.py:38
  1504.8 72.9 %reduce-scatter.14.cloned.1.call-start = ((), (), s32[]{:S(2)}) async-start(), calls=%async_computation.16 | async-start | bytes 2359296 | tf_op jit(solution)/shard_map/while/body/eval_jaxpr/reduce_scatter | solution.py:30
  1552.1 72.0 %reduce-scatter.16.cloned.1.call-start = ((), (), s32[]{:S(2)}) async-start(), calls=%async_computation.17 | async-start | bytes 983040 | tf_op jit(solution)/shard_map/while/body/eval_jaxpr/reduce_scatter | solution.py:38
  1637.3 74.9 %reduce-scatter.20.cloned.1.call-start = ((), (), s32[]{:S(2)}) async-start(), calls=%async_computation.19 | async-start | bytes 983040 | tf_op jit(solution)/shard_map/while/body/eval_jaxpr/reduce_scatter | solution.py:38
  1840.0 74.0 %reduce-scatter.20.cloned.1.call-start = ((), (), s32[]{:S(2)}) async-start(), calls=%async_computation.19 | async-start | bytes 983040 | tf_op jit(solution)/shard_map/while/body/eval_jaxpr/reduce_scatter | solution.py:38
  2041.8 74.0 %reduce-scatter.20.cloned.1.call-start = ((), (), s32[]{:S(2)}) async-start(), calls=%async_computation.19 | async-start | bytes 983040 | tf_op jit(solution)/shard_map/while/body/eval_jaxpr/reduce_scatter | solution.py:38
  2243.6 74.0 %reduce-scatter.20.cloned.1.call-start = ((), (), s32[]{:S(2)}) async-start(), calls=%async_computation.19 | async-start | bytes 983040 | tf_op jit(solution)/shard_map/while/body/eval_jaxpr/reduce_scatter | solution.py:38
  2445.3 74.0 %reduce-scatter.20.cloned.1.call-start = ((), (), s32[]{:S(2)}) async-start(), calls=%async_computation.19 | async-start | bytes 983040 | tf_op jit(solution)/shard_map/while/body/eval_jaxpr/reduce_scatter | solution.py:38
  2647.1 74.1 %reduce-scatter.20.cloned.1.call-start = ((), (), s32[]{:S(2)}) async-start(), calls=%async_computation.19 | async-start | bytes 983040 | tf_op jit(solution)/shard_map/while/body/eval_jaxpr/reduce_scatter | solution.py:38
  2849.0 74.0 %reduce-scatter.20.cloned.1.call-start = ((), (), s32[]{:S(2)}) async-start(), calls=%async_computation.19 | async-start | bytes 983040 | tf_op jit(solution)/shard_map/while/body/eval_jaxpr/reduce_scatter | solution.py:38
  3050.7 74.1 %reduce-scatter.20.cloned.1.call-start = ((), (), s32[]{:S(2)}) async-start(), calls=%async_computation.19 | async-start | bytes 983040 | tf_op jit(solution)/shard_map/while/body/eval_jaxpr/reduce_scatter | solution.py:38
  3316.2 78.3 %all-to-all-start.3 = ((bf16[8,4,256,96]{2,3,0,1:T(8,128)(2,1)}), bf16[8,4,256,96]{2,3,0,1:T(8,128)(2,1)S(1)}, u32[]{:S(2)}, u32[]{:S(2)}) async-start(bf16[8,4,256,96]{2,3,0,1:T(8,128)(2,1)} %get-tuple-element.1721), calls=%async_computation.12 | async-start | bytes 3145728 | tf_op jit(solution)/shard_map/all_to_all | solution.py:446
  3395.6 118.3 %all-to-all-start.1 = ((bf16[8,4,256,96]{2,3,0,1:T(8,128)(2,1)}), bf16[8,4,256,96]{2,3,0,1:T(8,128)(2,1)}, u32[]{:S(2)}, u32[]{:S(2)}) async-start(bf16[8,4,256,96]{2,3,0,1:T(8,128)(2,1)} %get-tuple-element.1713), calls=%async_computation.10 | async-start | bytes 3145728 | tf_op jit(solution)/shard_map/all_to_all | solution.py:445
  3400.7 104.8 %all-reduce.30.cloned.1.call-start = ((), (), s32[]{:S(2)}) async-start(), calls=%async_computation.13 | async-start | bytes 3538944 | tf_op jit(solution)/shard_map/psum | solution.py:423
  (425 other events, 8263.2 us)
Sparse Core Ops, SparseCore 0:
  170.9 23.4 reduce-scatter.11
  218.1 25.4 reduce-scatter.13
  266.7 23.2 reduce-scatter.15
  361.5 23.4 reduce-scatter.11
  408.7 25.4 reduce-scatter.13
  457.3 23.2 reduce-scatter.15
  552.1 23.4 reduce-scatter.11
  599.3 25.5 reduce-scatter.13
  742.7 23.4 reduce-scatter.11
  789.9 25.5 reduce-scatter.13
  933.3 23.4 reduce-scatter.11
  980.5 25.5 reduce-scatter.13
  1123.8 23.4 reduce-scatter.11
  1171.0 25.5 reduce-scatter.13
  1314.4 23.4 reduce-scatter.11
  1361.6 25.5 reduce-scatter.13
  1410.2 23.2 reduce-scatter.15
  1504.9 23.5 reduce-scatter.11
  1552.2 25.4 reduce-scatter.13
  1600.7 23.2 reduce-scatter.15
  1637.4 26.3 reduce-scatter.17
  1688.9 23.2 reduce-scatter.19
  1840.1 25.4 reduce-scatter.17
  1890.7 23.3 reduce-scatter.19
  2041.9 25.4 reduce-scatter.17
  2243.7 25.4 reduce-scatter.17
  2445.5 25.4 reduce-scatter.17
  2647.3 25.5 reduce-scatter.17
  2697.8 23.3 reduce-scatter.19
  2849.1 25.4 reduce-scatter.17
  3050.9 25.5 reduce-scatter.17
  3101.4 23.2 reduce-scatter.19
  (40 shorter events, 769.8 us)
Sparse Core Ops, SparseCore 1:
  3405.0 99.6 all-reduce.29
where the time goes:
time: 3540 us; the launch traced here: 3530 us
  waiting for transfers between devices  1350 us (38%)
  blocking collectives  1250 us (35%)
  other arithmetic  350 us (10%)
  local copies, waits for them, and re-layouts  290 us (8%)
  matrix products  240 us (7%)
    reduce_scatter x40, waiting for transfers between devices, token_scatter(): return lax.psum_scatter(values, 'row', scatter_dimension=0, tiled=True)  684 us
    reduce_scatter x32, waiting for transfers between devices, feature_scatter(): return lax.psum_scatter(values, 'col', scatter_dimension=1, tiled=True)  594 us
    psum x32, blocking collectives, wide_sums(): return lax.psum(partials, ('row', 'col'))  406 us
    all_gather x40, blocking collectives, token_gather(): return lax.all_gather(values, 'row', axis=0, tiled=True)  343 us
    psum x32, blocking collectives, narrow_sums(): return lax.psum(partials, 'col')  210 us
    all_gather x32, blocking collectives, feature_gather(): return lax.all_gather(values, 'col', axis=1, tiled=True)  197 us
    dynamic_update_slice x112, local copies, waits for them, and re-layouts, body(): lax.scan(forward_step, jnp.zeros((), jnp.float32), (in_units, segments))  122 us
    scatter x96, local copies, waits for them, and re-layouts  79.5 us
  transfers between devices with their start and end apart: 77, of which 74 were waited for; matrix products, arithmetic and copies ran while one was open for 11% of the time, Pallas kernels for 0%

commit v1 on v0

v1 whole, which is shorter than its diff:
```python
import math

import jax
import jax.numpy as jnp
from jax import lax
from jax.sharding import PartitionSpec as P

HEAD = 64
eps = 1e-05
masked_score = -1e30
f32 = jnp.float32
bf16 = jnp.bfloat16
RC = ("row", "col")


def mm(spec, a, b):
    return jnp.einsum(spec, a, b, preferred_element_type=f32)


def norm(v, gain, shift):
    mu = jnp.mean(v, axis=0, keepdims=True)
    d = v - mu
    r = lax.rsqrt(jnp.mean(d * d, axis=0, keepdims=True) + eps)
    vh = d * r
    return vh * gain + shift, vh, r


def norm_back(up, vh, r, gain):
    h = up * gain
    m1 = jnp.mean(h, axis=0, keepdims=True)
    m2 = jnp.mean(h * vh, axis=0, keepdims=True)
    return (
        r * (h - m1 - vh * m2),
        jnp.sum(up * vh, axis=1, keepdims=True),
        jnp.sum(up, axis=1, keepdims=True),
    )


def scores_of(q, k, visible):
    s = mm("hek,heq->hkq", k, q) * (1.0 / math.sqrt(HEAD))
    return jnp.where(visible[None], s, masked_score)


def body(
    tokens,
    cotangent,
    holder_of,
    lengths,
    input_gain,
    input_shift,
    attend_weight,
    attend_bias,
    mixed_gain,
    mixed_shift,
    output_weight,
    output_bias,
    middle_gain,
    middle_shift,
    expand_weight,
    expand_bias,
    hidden_gain,
    hidden_shift,
    shrink_weight,
    shrink_bias,
):
    holders = lax.axis_size("dp")
    half = holders // 2
    nr, nc = lax.axis_size("row"), lax.axis_size("col")
    n = nr * nc
    micro = holder_of.shape[0]
    assert micro == n
    fl = tokens.shape[0]
    pairs = micro * half
    blk = tokens.shape[1] // pairs
    unit = half * blk
    dp = lax.axis_index("dp")
    side, pos = dp // half, dp % half
    rc = lax.axis_index("row") * nc + lax.axis_index("col")
    groups = [[s * half + p for p in range(half)] for s in range(2)]

    def to_unit(v):
        v = v.reshape(fl, half, n, blk)
        v = jnp.transpose(v, (1, 2, 0, 3))
        v = lax.all_to_all(v, "dp", 0, 0, axis_index_groups=groups, tiled=True)
        v = jnp.transpose(v, (1, 2, 0, 3)).reshape(n, fl, unit)
        v = lax.all_to_all(v, RC, 0, 0, tiled=True)
        return v.reshape(n * fl, unit)

    def from_unit(v):
        v = lax.all_to_all(v.reshape(n, fl, unit), RC, 0, 0, tiled=True)
        v = jnp.transpose(v.reshape(n, fl, half, blk), (2, 0, 1, 3))
        v = lax.all_to_all(v, "dp", 0, 0, axis_index_groups=groups, tiled=True)
        return jnp.transpose(v, (2, 0, 1, 3)).reshape(tokens.shape)

    def gather(v):
        return lax.all_gather(v, RC, axis=0)

    ga = gather(attend_weight)
    go = gather(output_weight)
    ge = gather(expand_weight)
    gs = gather(shrink_weight)
    hw, rw, fw = output_weight.shape[0], output_weight.shape[1], shrink_weight.shape[0]

    thin = jnp.concatenate(
        [
            v.reshape(-1)
            for v in (
                input_gain, input_shift, output_bias, middle_gain, middle_shift, shrink_bias,
                attend_bias, mixed_gain, mixed_shift, expand_bias, hidden_gain, hidden_shift,
            )
        ]
    )
    thin = lax.all_gather(thin, RC, axis=0)
    sizes = [fl] * 6 + [hw] * 4 + [fw] * 3
    cols, at = [], 0
    for i, size in enumerate(sizes):
        piece = thin[:, at : at + size] if i < 6 else thin[:nc, at : at + size]
        cols.append(piece.reshape(-1, 1))
        at += size
    in_g, in_s, out_b, mid_g, mid_s, shr_b, q_b, v_b, mix_g, mix_s, exp_b, hid_g, hid_s = cols

    k_unit = 2 * (pos * n + rc) + side
    m_of, u_of = k_unit // holders, k_unit % holders
    own = lengths[m_of, holder_of[m_of, u_of]]
    bounds = jnp.cumsum(own)[:-1]
    at_row = jnp.arange(unit, dtype=jnp.int32)
    segment = jnp.sum((at_row[:, None] >= bounds[None, :]).astype(jnp.int32), axis=1)
    visible = segment[:, None] == segment[None, :]

    x = to_unit(tokens).astype(f32)
    e2 = to_unit(cotangent)

    a, vh_in, r_in = norm(x, in_g, in_s)
    a = a.astype(bf16)
    gar = ga.reshape(nr, nc, 3, hw, rw)
    trip = mm("rcjif,rft->jcit", gar, a.reshape(nr, rw, unit)).reshape(3, nc * hw, unit)
    heads = lambda v: v.reshape(-1, HEAD, unit)
    q = heads((trip[0] + q_b).astype(bf16))
    k = heads(trip[1].astype(bf16))
    v = heads((trip[2] + v_b).astype(bf16))
    s = scores_of(q, k, visible)
    top = jnp.max(s, axis=1, keepdims=True)
    ex = jnp.exp(s - top)
    den = jnp.sum(ex, axis=1, keepdims=True)
    prob = ex / den
    o = mm("hek,hkq->heq", v, prob.astype(bf16)).reshape(nc * hw, unit)
    on, vh_mix, r_mix = norm(o, mix_g, mix_s)
    on = on.astype(bf16)
    gor = go.reshape(nr, nc * hw, rw)
    x1 = x + mm("rin,it->rnt", gor, on).reshape(nr * rw, unit) + out_b
    b, vh_mid, r_mid = norm(x1, mid_g, mid_s)
    b = b.astype(bf16)
    ger = ge.reshape(nr, nc, rw, fw)
    f = mm("rckn,rkt->cnt", ger, b.reshape(nr, rw, unit)).reshape(nc * fw, unit) + exp_b
    phi = 0.5 * (1.0 + lax.erf(f * math.sqrt(0.5)))
    g = f * phi
    gn, vh_hid, r_hid = norm(g, hid_g, hid_s)
    gn = gn.astype(bf16)
    gsr = gs.reshape(nr, nc * fw, rw)
    y = x1 + mm("rfn,ft->rnt", gsr, gn).reshape(nr * rw, unit) + shr_b
    block_out = from_unit(y.astype(bf16))

    e2r = e2.reshape(nr, rw, unit)
    d_shr_w = mm("cft,rdt->rcfd", gn.reshape(nc, fw, unit), e2r).astype(bf16)
    dy = e2.astype(f32)
    d_shr_b = jnp.sum(dy, axis=1, keepdims=True)
    dgn = mm("rfd,rdt->ft", gsr, e2r)
    dg, d_hid_g, d_hid_s = norm_back(dgn, vh_hid, r_hid, hid_g)
    slope = phi + f * (jnp.exp(-0.5 * f * f) * (1.0 / math.sqrt(2.0 * math.pi)))
    df = (dg * slope).astype(bf16)
    d_exp_b = jnp.sum(df.astype(f32), axis=1, keepdims=True)
    dfc = df.reshape(nc, fw, unit)
    d_exp_w = mm("rkt,cnt->rckn", b.reshape(nr, rw, unit), dfc).astype(bf16)
    db = mm("rckn,cnt->rkt", ger, dfc).reshape(nr * rw, unit)
    dx1, d_mid_g, d_mid_s = norm_back(db, vh_mid, r_mid, mid_g)
    dx1 = dy + dx1
    e1 = dx1.astype(bf16)
    d_out_b = jnp.sum(e1.astype(f32), axis=1, keepdims=True)
    e1r = e1.reshape(nr, rw, unit)
    d_out_w = mm("cit,rnt->rcin", on.reshape(nc, hw, unit), e1r).astype(bf16)
    don = mm("rin,rnt->it", gor, e1r)
    do, d_mix_g, d_mix_s = norm_back(don, vh_mix, r_mix, mix_g)
    do = heads(do.astype(bf16))
    dprob = mm("hek,heq->hkq", v, do)
    inner = jnp.sum(prob * dprob, axis=1, keepdims=True)
    ds = (prob * (dprob - inner)).astype(bf16)
    scale = 1.0 / math.sqrt(HEAD)
    dq = (mm("hek,hkq->heq", k, ds) * scale).astype(bf16).reshape(nc, hw, unit)
    dk = (mm("heq,hkq->hek", q, ds) * scale).astype(bf16).reshape(nc, hw, unit)
    dv = mm("heq,hkq->hek", do, prob.astype(bf16)).astype(bf16).reshape(nc, hw, unit)
    d_q_b = jnp.sum(dq.astype(f32), axis=2)
    d_v_b = jnp.sum(dv.astype(f32), axis=2)
    dtrip = jnp.stack([dq, dk, dv], axis=1)
    d_att_w = mm("cjit,rft->rcjif", dtrip, a.reshape(nr, rw, unit)).astype(bf16)
    da = mm("rcjif,cjit->rft", gar, dtrip).reshape(nr * rw, unit)
    dx, d_in_g, d_in_s = norm_back(da, vh_in, r_in, in_g)
    input_grad = from_unit((dx1 + dx).astype(bf16))

    def reduce(v):
        v = v.reshape((n,) + v.shape[2:])
        return lax.psum(lax.psum_scatter(v, RC, scatter_dimension=0, tiled=False), "dp")

    shr_w_g = reduce(d_shr_w).astype(f32)
    exp_w_g = reduce(d_exp_w).astype(f32)
    out_w_g = reduce(d_out_w).astype(f32)

    by_rc = [v.reshape(n, fl) for v in (d_in_g, d_in_s, d_out_b, d_mid_g, d_mid_s, d_shr_b)]
    by_c = [
        jnp.broadcast_to(v.reshape(1, nc, -1), (nr, nc, v.size // nc)).reshape(n, -1)
        for v in (d_q_b, d_v_b, d_mix_g, d_mix_s, d_exp_b, d_hid_g, d_hid_s)
    ]
    small = jnp.concatenate(by_rc + by_c, axis=1).astype(bf16)
    width = small.shape[1]
    pad = -width % rw
    small = jnp.pad(small, ((0, 0), (0, pad))).reshape(nr, nc, -1, rw)
    last = jnp.concatenate([d_att_w.reshape(nr, nc, 3 * hw, rw), small], axis=2)
    last = reduce(last).astype(f32)
    att_w_g = last[: 3 * hw].reshape(attend_weight.shape)
    flat = last[3 * hw :].reshape(-1)
    outs, at = [], 0
    for size in sizes:
        outs.append(flat[at : at + size])
        at += size
    in_g_g, in_s_g, out_b_g, mid_g_g, mid_s_g, shr_b_g, q_b_g, v_b_g, mix_g_g, mix_s_g, exp_b_g, hid_g_g, hid_s_g = outs
    return (
        block_out,
        input_grad,
        in_g_g,
        in_s_g,
        att_w_g,
        jnp.stack([q_b_g, v_b_g]),
        mix_g_g,
        mix_s_g,
        out_w_g,
        out_b_g,
        mid_g_g,
        mid_s_g,
        exp_w_g,
        exp_b_g,
        hid_g_g,
        hid_s_g,
        shr_w_g,
        shr_b_g,
    )


def solution(mesh):
    wide, narrow = P(RC), P("col")
    in_specs = (
        P(RC, "dp"), P(RC, "dp"), P(), P(), wide, wide, P(None, "col", "row"), P(None, "col"),
        narrow, narrow, P("col", "row"), wide, wide, wide, P("row", "col"), narrow, narrow, narrow,
        P("col", "row"), wide,
    )
    out_specs = (
        P(RC, "dp"), P(RC, "dp"), wide, wide, P(None, "col", "row"), P(None, "col"), narrow, narrow,
        P("col", "row"), wide, wide, wide, P("row", "col"), narrow, narrow, narrow, P("col", "row"),
        wide,
    )
    return jax.shard_map(body, mesh=mesh, in_specs=in_specs, out_specs=out_specs, check_vma=False)
```

time: 3540 us -> 613 us (0.17)
  blocking collectives: 1250 us -> 20.6 us
  waiting for transfers between devices: 1350 us -> 337 us
  other arithmetic: 350 us -> 44.9 us
  local copies, waits for them, and re-layouts: 290 us -> 60.3 us
  matrix products: 240 us -> 99.4 us
    reduce_scatter x72 -> x4, waiting for transfers between devices: 1280 us -> 133 us  [reduce(): lax.psum_scatter(v, RC, scatter_dimension=0, tiled=False)]
    psum x66 -> x0, blocking collectives: 714 us -> none  [the longest x32 406 us: wide_sums(): return lax.psum(partials, ('row', 'col'))]
    all_gather x72 -> x0, blocking collectives: 540 us -> none  [the longest x40 343 us: token_gather(): return lax.all_gather(values, 'row', axis=0, tiled=True)]
    dot_general x156 -> x17, matrix products: 240 us -> 88.7 us  [mm(): return jnp.einsum(spec, a, b, preferred_element_type=f32)]
    reduce_sum x114 -> x11, other arithmetic: 152 us -> 18.6 us  [the longest x1 7.74 us: body(): d_exp_b = jnp.sum(df.astype(f32), axis=1, keepdims=True)]
    dynamic_update_slice x112 -> x0, local copies, waits for them, and re-layouts: 122 us -> none  [body(): lax.scan(forward_step, jnp.zeros((), jnp.float32), (in_units, segments))]
    all_gather x0 -> x4, waiting for transfers between devices: none -> 88.1 us  [gather(): return lax.all_gather(v, RC, axis=0)]
    scatter x96 -> x0, local copies, waits for them, and re-layouts: 79.5 us -> none
  transfers between devices with their start and end apart: 77 -> 17, of which waited for: 74 -> 12; matrix products, arithmetic and copies ran while one was open for 11% -> 21% of each run, Pallas kernels for 0% -> 0%
where the time goes in v1:
time: 613 us; the launch traced here: 607 us
  waiting for transfers between devices  337 us (55%)
  matrix products  99.4 us (16%)
  local copies, waits for them, and re-layouts  60.3 us (10%)
  other arithmetic  44.9 us (7%)
  starting transfers between devices  27.1 us (4%)
  blocking collectives  20.6 us (3%)
  between operations  18.1 us (3%)
    reduce_scatter x4, waiting for transfers between devices, reduce(): lax.psum_scatter(v, RC, scatter_dimension=0, tiled=False)  133 us
    dot_general x17, matrix products, mm(): return jnp.einsum(spec, a, b, preferred_element_type=f32)  88.7 us
    all_gather x4, waiting for transfers between devices, gather(): return lax.all_gather(v, RC, axis=0)  88.1 us
    all_to_all x2, waiting for transfers between devices, from_unit(): v = lax.all_to_all(v, 'dp', 0, 0, axis_index_groups=groups, tiled=True)  42.4 us
    psum x1, waiting for transfers between devices, reduce(): lax.psum(lax.psum_scatter(v, RC, scatter_dimension=0, tiled=False), 'dp')  38.5 us
    unnamed x11, waiting for transfers between devices  20.7 us
    all_to_all x1, blocking collectives, from_unit(): v = lax.all_to_all(v.reshape(n, fl, unit), RC, 0, 0, tiled=True)  20.6 us
    all_to_all x2, waiting for transfers between devices, to_unit(): v = lax.all_to_all(v, 'dp', 0, 0, axis_index_groups=groups, tiled=True)  14.4 us
  transfers between devices with their start and end apart: 17, of which 12 were waited for; matrix products, arithmetic and copies ran while one was open for 21% of the time, Pallas kernels for 0%

profile of v1, /device:TPU:0, one launch (start us, length us, event | category | flops | bytes accessed | tf_op | source)
XLA Modules:
  0.0 607.3 jit_solution(13611442720965010342)
XLA Ops:
  15.2 4.3 all-to-all-start
  20.6 10.5 %all-to-all-done = bf16[2,8,96,256]{3,1,2,0:T(8,128)(2,1)S(1)} async-done(((bf16[2,8,96,256]{3,1,2,0:T(8,128)(2,1)}), bf16[2,8,96,256]{3,1,2,0:T(8,128)(2,1)S(1)}, u32[]{:S(2)}, u32[]{:S(2)}) %all-to-all-start) | async-done | bytes 786464 | tf_op jit(solution)/shard_map/all_to_all | solution.py:84
  48.9 18.1 %all-reduce.6.cloned.1.call-done = f32[29184]{0:T(1024)} async-done(((f32[29184]{0:T(1024)}), f32[29184]{0:T(1024)}) %all-reduce.6.cloned.1.call-update) | async-done | bytes 116752
  73.3 4.2 all-to-all-start.5
  79.0 32.5 %all-gather.10.cloned.1.call-done = bf16[24,192,384]{2,1,0:T(8,128)(2,1)} async-done(((bf16[3,192,384]{2,1,0:T(8,128)(2,1)}), bf16[24,192,384]{2,1,0:T(8,128)(2,1)}) %all-gather.10.cloned.1.call-update) | async-done | bytes 3538960 | tf_op jit(solution)/shard_map/all_gather | solution.py:96
  111.5 4.1 convolution_bitcast_fusion.1
  117.9 10.7 %fusion.64 = (f32[12,512]{1,0:T(8,128)S(1)}, f32[12,512,512]{2,1,0:T(8,128)}) fusion(pred[512,512]{1,0:T(8,128)(4,1)S(1)} %broadcast_compare_fusion, bf16[12,64,512]{2,1,0:T(8,128)(2,1)S(1)} %bitcast.299, f32[12,64,512]{2,1,0:T(8,128)} %bitcast.302, f32[12,64]{1,0:T(8,128)S(1)} %add.260), kind=kOutput, calls=%fused_computation.139 | convolution fusion | flops 416023040 | bytes 15232000 | tf_op jit(solution)/shard_map/sub | solution.py:143
  128.6 6.6 %fusion.65 = (f32[512]{0:T(512)S(1)}, f32[12,64,512]{2,1,0:T(8,128)S(1)}) fusion(f32[12,512,512]{2,1,0:T(8,128)} %get-tuple-element.76, f32[12,512]{1,0:T(8,128)S(1)} %get-tuple-element.75, f32[12,64,512]{2,1,0:T(8,128)} %bitcast.321, f32[12,64]{1,0:T(8,128)S(1)} %add.249), kind=kOutput, calls=%fused_computation.140 | convolution fusion | flops 410123776 | bytes 15758336 | tf_op jit(solution)/shard_map/hek,hkq->heq/dot_general | solution.py:17
  144.4 34.1 %all-gather.14.cloned.1.call-done = bf16[3072,768]{1,0:T(8,128)(2,1)} async-done(((bf16[384,768]{1,0:T(8,128)(2,1)}), bf16[3072,768]{1,0:T(8,128)(2,1)}) %all-gather.14.cloned.1.call-update) | async-done | bytes 4718608 | tf_op jit(solution)/shard_map/all_gather | solution.py:96
  178.5 9.1 %fusion.54 = (f32[512]{0:T(512)S(1)}, f32[4,768,512]{1,2,0:T(8,128)}, f32[4,768,512]{1,2,0:T(8,128)}) fusion(f32[4,768]{1,0:T(4,128)S(1)} %get-tuple-element.57, bf16[2,4,384,768]{3,2,1,0:T(8,128)(2,1)} %bitcast.344, f32[2,384]{1,0:T(2,128)S(1)} %add.275, f32[2,384]{1,0:T(2,128)S(1)} %mul.381, f32[512]{0:T(512)S(1)} %add_rsqrt_fusion.1, ...), kind=kOutput, calls=%fused_computation.130 | convolution fusion | flops 2427321856 | bytes 18898944 | tf_op jit(solution)/shard_map/rckn,rkt->cnt/dot_general | solution.py:17
  187.6 6.7 %copy.132 = f32[4,768,512]{2,1,0:T(8,128)} copy(f32[4,768,512]{1,2,0:T(8,128)} %get-tuple-element.79) | data formatting | bytes 12582912 | tf_op jit(solution)/shard_map/rckn,rkt->cnt/dot_general | solution.py:17
  197.8 21.5 %all-gather.16.cloned.1.call-done = bf16[6144,384]{1,0:T(8,128)(2,1)} async-done(((bf16[768,384]{1,0:T(8,128)(2,1)}), bf16[6144,384]{1,0:T(8,128)(2,1)}) %all-gather.16.cloned.1.call-update) | async-done | bytes 4718608 | tf_op jit(solution)/shard_map/all_gather | solution.py:96
  219.3 8.5 %fusion.8 = (bf16[3072]{0:T(1024)(128)(2,1)S(1)}, f32[512]{0:T(512)S(1)}, f32[512]{0:T(512)S(1)}, bf16[3072]{0:T(1024)(128)(2,1)S(1)}, f32[3072,512,1]{1,0,2:T(8,128)S(1)}) fusion(f32[4,768,512]{2,1,0:T(8,128)} %copy.132, f32[512]{0:T(512)S(1)} %broadcast_multiply_fusion.2, f32[3072]{0:T(1024)S(1)} %add.288, f32[512]{0:T(512)S(1)} %add_rsqrt_fusion, ...), kind=kOutput, calls=%fused_computation.17 | convolution fusion | flops 2437932032 | bytes 18132992 | tf_op jit(solution)/shard_map/rfd,rdt->ft/dot_general | solution.py:17
  227.9 7.7 %fusion.52 = (bf16[3072]{0:T(1024)(128)(2,1)S(1)}, bf16[3072,512]{1,0:T(8,128)(2,1)S(1)}) fusion(f32[512]{0:T(512)S(1)} %get-tuple-element.89, f32[512]{0:T(512)S(1)} %broadcast_multiply_fusion.2, f32[3072]{0:T(1024)S(1)} %add.288, f32[4,768,512]{2,1,0:T(8,128)S(1)} %bitcast.285, f32[512]{0:T(512)S(1)} %get-tuple-element.90, f32[3072]{0:T(1024)S(1)} %mul.396, ...), kind=kLoop, calls=%fused_computation.129 | loop fusion | flops 31454208 | bytes 15767552 | tf_op jit(solution)/shard_map/reduce_sum | solution.py:171
  235.6 6.0 fusion.30
  249.3 7.9 %fusion.67 = (bf16[12,64]{1,0:T(8,128)(2,1)S(1)}, bf16[12,64,512]{2,1,0:T(8,128)(2,1)}) fusion(bf16[12,64,512]{2,1,0:T(8,128)(2,1)} %bitcast.331, f32[12,512,512]{2,1,0:T(8,128)} %get-tuple-element.76, f32[12,512]{1,0:T(8,128)S(1)} %get-tuple-element.75), kind=kOutput, calls=%fused_computation.142 | convolution fusion | flops 409730304 | bytes 14181888 | tf_op jit(solution)/shard_map/heq,hkq->hek/dot_general | solution.py:17
  257.2 8.9 %multiply_reduce_fusion = (f32[12,512]{1,0:T(8,128)S(1)}, f32[12,512,512]{2,1,0:T(8,128)}) fusion(f32[12,512,512]{2,1,0:T(8,128)} %get-tuple-element.76, f32[12,512]{1,0:T(8,128)S(1)} %get-tuple-element.75, bf16[12,64,512]{2,1,0:T(8,128)(2,1)S(1)} %bitcast.332, f32[12,64,512]{2,1,0:T(8,128)S(1)} %bitcast.322, f32[12,64]{1,0:T(8,128)S(1)} %add.249), kind=kOutput, calls=%fused_computation.2 | convolution fusion | flops 412870656 | bytes 27577344 | tf_op jit(solution)/shard_map/hek,heq->hkq/dot_general | solution.py:17
  266.1 6.4 %multiply_convert_fusion = bf16[12,512,512]{2,1,0:T(8,128)(2,1)S(1)} fusion(f32[12,512,512]{2,1,0:T(8,128)} %get-tuple-element.84, f32[12,512]{1,0:T(8,128)S(1)} %get-tuple-element.83, f32[12,512,512]{2,1,0:T(8,128)S(1)} %bitcast.298, f32[12,512]{1,0:T(8,128)S(1)} %get-tuple-element.75), kind=kLoop, calls=%fused_computation.1 | loop fusion | flops 12582912 | bytes 31506432 | tf_op jit(solution)/shard_map/convert_element_type | solution.py:186
  279.3 6.0 fusion.22
  299.4 4.0 add_convert_fusion
  305.1 4.3 convert_bitcast_fusion
  313.4 7.2 %convert_bitcast_fusion.1 = bf16[2,4,384,768]{2,3,0,1:T(8,128)(2,1)} fusion(bf16[4,768,512,1]{2,1,3,0:T(8,128)(2,1)} %bitcast.317, f32[2,384,512]{2,1,0:T(8,128)S(1)} %copy-done.10, f32[2,384]{1,0:T(2,128)S(1)} %add.275, f32[2,384]{1,0:T(2,128)S(1)} %mul.381, f32[512]{0:T(512)S(1)} %add_rsqrt_fusion.1, f32[512]{0:T(512)S(1)} %broadcast_multiply_fusion.9), kind=kOutput, calls=%fused_computation.30 | convolution fusion | flops 2420244480 | bytes 9447424 | tf_op jit(solution)/shard_map/rkt,cnt->rckn/dot_general | solution.py:17
  320.6 6.7 %copy.143 = bf16[2,4,384,768]{3,2,1,0:T(8,128)(2,1)} copy(bf16[2,4,384,768]{2,3,0,1:T(8,128)(2,1)} %convert_bitcast_fusion.1) | data formatting | bytes 9437184 | tf_op jit(solution)/shard_map/convert_element_type | solution.py:173
  327.3 4.8 copy.126
  332.2 5.8 fusion.69
  341.2 20.6 %all_to_all.40 = bf16[8,96,512]{2,1,0:T(8,128)(2,1)S(1)} all-to-all(bf16[8,96,512]{2,1,0:T(8,128)(2,1)S(1)} %get-tuple-element.47), channel_id=1, replica_groups=mesh['dp'=4,'row'=2,'col'=4] {'row','col'}, dimensions={0} | all-to-all | bytes 1572864 | tf_op jit(solution)/shard_map/all_to_all | solution.py:90
  365.4 17.6 %reduce-scatter.5.cloned.1.call-done = bf16[1,586,384]{2,1,0:T(8,128)(2,1)} async-done(((bf16[8,586,384]{2,1,0:T(8,128)(2,1)}), bf16[1,586,384]{2,1,0:T(8,128)(2,1)}) %reduce-scatter.5.cloned.1.call-update) | async-done | bytes 450064 | tf_op jit(solution)/shard_map/reduce_scatter | solution.py:201
  383.0 57.8 %reduce-scatter.11.cloned.1.call-done = bf16[1,768,384]{2,1,0:T(8,128)(2,1)} async-done(((bf16[8,768,384]{2,1,0:T(8,128)(2,1)}), bf16[1,768,384]{2,1,0:T(8,128)(2,1)}) %reduce-scatter.11.cloned.1.call-update) | async-done | bytes 589840 | tf_op jit(solution)/shard_map/reduce_scatter | solution.py:201
  440.8 57.4 %reduce-scatter.9.cloned.1.call-done = bf16[1,384,768]{2,1,0:T(8,128)(2,1)} async-done(((bf16[8,384,768]{2,1,0:T(8,128)(2,1)}), bf16[1,384,768]{2,1,0:T(8,128)(2,1)}) %reduce-scatter.9.cloned.1.call-update) | async-done | bytes 589840 | tf_op jit(solution)/shard_map/reduce_scatter | solution.py:201
  504.8 26.5 %all-to-all-done.7 = bf16[2,8,96,256]{3,1,2,0:T(8,128)(2,1)S(1)} async-done(((bf16[2,8,96,256]{3,1,2,0:T(8,128)(2,1)}), bf16[2,8,96,256]{3,1,2,0:T(8,128)(2,1)S(1)}, u32[]{:S(2)}, u32[]{:S(2)}) %all-to-all-start.7) | async-done | bytes 786464 | tf_op jit(solution)/shard_map/all_to_all | solution.py:92
  536.1 15.9 %all-to-all-done.3 = bf16[2,8,96,256]{3,1,2,0:T(8,128)(2,1)S(1)} async-done(((bf16[2,8,96,256]{3,1,2,0:T(8,128)(2,1)}), bf16[2,8,96,256]{3,1,2,0:T(8,128)(2,1)S(1)}, u32[]{:S(2)}, u32[]{:S(2)}) %all-to-all-start.3) | async-done | bytes 786464 | tf_op jit(solution)/shard_map/all_to_all | solution.py:92
  553.2 38.5 %all-reduce.8.cloned.1.call-done = (bf16[586,384]{1,0:T(8,128)(2,1)}, bf16[192,384]{1,0:T(8,128)(2,1)}, bf16[384,768]{1,0:T(8,128)(2,1)}, bf16[768,384]{1,0:T(8,128)(2,1)}) async-done(((bf16[586,384]{1,0:T(8,128)(2,1)}, bf16[192,384]{1,0:T(8,128)(2,1)}, bf16[384,768]{1,0:T(8,128)(2,1)}, bf16[768,384]{1,0:T(8,128)(2,1)}), (bf16[586,384]{1,0:T(8,128)(2,1)}, bf16[192,384]{1,0:T(8,128)(2,1)}, ...) | async-done | bytes 1777168 | tf_op jit(solution)/shard_map/psum | solution.py:201
  (267 shorter events, 108.4 us)
Async XLA Ops:
  7.2 31.3 %copy-start = (s32[8,4,4]{0,2,1:T(4,128)S(1)}, s32[8,4,4]{0,2,1:T(4,128)}, u32[]{:S(2)}) copy-start(s32[8,4,4]{0,2,1:T(4,128)} %param.23) | copy-start | bytes 1540
  7.2 6.9 %copy-start.23 = (bf16[96,4096]{1,0:T(8,128)(2,1)S(1)}, bf16[96,4096]{1,0:T(8,128)(2,1)}, u32[]{:S(2)}) copy-start(bf16[96,4096]{1,0:T(8,128)(2,1)} %param.20) | copy-start | bytes 2359300
  7.2 59.8 %all-reduce.6.cloned.1.call-start = ((), (), s32[]{:S(2)}) async-start(), calls=%async_computation.20 | async-start | bytes 237568
  12.0 99.5 %all-gather.10.cloned.1.call-start = ((), (), s32[]{:S(2)}) async-start(), calls=%async_computation.16 | async-start | bytes 3981312 | tf_op jit(solution)/shard_map/all_gather | solution.py:96
  12.8 125.5 %all-gather.12.cloned.1.call-start = ((), (), s32[]{:S(2)}) async-start(), calls=%async_computation.17 | async-start | bytes 1327104 | tf_op jit(solution)/shard_map/all_gather | solution.py:96
  13.5 165.0 %all-gather.14.cloned.1.call-start = ((), (), s32[]{:S(2)}) async-start(), calls=%async_computation.18 | async-start | bytes 5308416 | tf_op jit(solution)/shard_map/all_gather | solution.py:96
  15.2 15.9 %all-to-all-start = ((bf16[2,8,96,256]{3,1,2,0:T(8,128)(2,1)}), bf16[2,8,96,256]{3,1,2,0:T(8,128)(2,1)S(1)}, u32[]{:S(2)}, u32[]{:S(2)}) async-start(bf16[2,8,96,256]{3,1,2,0:T(8,128)(2,1)} %copy.120), calls=%async_computation | async-start | bytes 1572864 | tf_op jit(solution)/shard_map/all_to_all | solution.py:84
  31.1 14.0 %all-to-all-start.4 = ((bf16[2,8,96,256]{3,1,2,0:T(8,128)(2,1)}), bf16[2,8,96,256]{3,1,2,0:T(8,128)(2,1)S(1)}, u32[]{:S(2)}, u32[]{:S(2)}) async-start(bf16[2,8,96,256]{3,1,2,0:T(8,128)(2,1)} %copy.130), calls=%async_computation.4 | async-start | bytes 1572864 | tf_op jit(solution)/shard_map/all_to_all | solution.py:84
  34.6 184.7 %all-gather.16.cloned.1.call-start = ((), (), s32[]{:S(2)}) async-start(), calls=%async_computation.19 | async-start | bytes 5308416 | tf_op jit(solution)/shard_map/all_gather | solution.py:96
  45.1 28.2 %all-to-all-start.1 = ((bf16[8,96,512]{2,1,0:T(8,128)(2,1)}), bf16[8,96,512]{2,1,0:T(8,128)(2,1)S(1)}, u32[]{:S(2)}, u32[]{:S(2)}) async-start(bf16[8,96,512]{2,1,0:T(8,128)(2,1)} %reshape.770), calls=%async_computation.1 | async-start | bytes 1572864 | tf_op jit(solution)/shard_map/all_to_all | solution.py:86
  69.4 9.3 %copy-start.46 = (f32[2,384]{1,0:T(2,128)}, f32[2,384]{1,0:T(2,128)S(1)}, u32[]{:S(2)}) copy-start(f32[2,384]{1,0:T(2,128)S(1)} %mul.364) | copy-start | bytes 9220
  73.3 124.6 %all-to-all-start.5 = ((bf16[8,96,512]{2,1,0:T(8,128)(2,1)}), bf16[8,96,512]{2,1,0:T(8,128)(2,1)}, u32[]{:S(2)}, u32[]{:S(2)}) async-start(bf16[8,96,512]{2,1,0:T(8,128)(2,1)} %reshape.782), calls=%async_computation.5 | async-start | bytes 1572864 | tf_op jit(solution)/shard_map/all_to_all | solution.py:86
  77.5 287.9 %reduce-scatter.7.cloned.1.call-start = ((), (), s32[]{:S(2)}) async-start(), calls=%async_computation.13 | async-start | bytes 1327104 | tf_op jit(solution)/shard_map/reduce_scatter | solution.py:201
  78.7 36.9 %copy-start.44 = (f32[512]{0:T(512)}, f32[512]{0:T(512)S(1)}, u32[]{:S(2)}) copy-start(f32[512]{0:T(512)S(1)} %add_rsqrt_fusion.3) | copy-start | bytes 6148
  79.0 32.5 %copy-start.26 = (bf16[2,384,512,1,1]{2,1,4,3,0:T(8,128)(2,1)}, bf16[2,384,512,1,1]{2,1,4,3,0:T(8,128)(2,1)S(1)}, u32[]{:S(2)}) copy-start(bf16[2,384,512,1,1]{2,1,4,3,0:T(8,128)(2,1)S(1)} %fusion.41) | copy-start | bytes 2359300
  219.3 8.5 %slice-start = ((s8[6291456]{0:T(1024)(128)(4,1)}), s8[4194304]{0:T(1024)(128)(4,1)S(1)}, s32[]{:S(2)}) async-start(s8[6291456]{0:T(1024)(128)(4,1)} %bitcast.284), calls=%async_computation.22 | async-start | bytes 8388608
  219.3 8.5 %slice-start.1 = ((s8[6291456]{0:T(1024)(128)(4,1)}), s8[2097152]{0:T(1024)(128)(4,1)S(1)}, s32[]{:S(2)}) async-start(s8[6291456]{0:T(1024)(128)(4,1)} %bitcast.284), calls=%async_computation.23 | async-start | bytes 4194304
  227.9 7.8 %copy-start.9 = (f32[2,384,512]{2,1,0:T(8,128)S(1)}, f32[2,384,512]{2,1,0:T(8,128)}, u32[]{:S(2)}) copy-start(f32[2,384,512]{2,1,0:T(8,128)} %copy-done.8) | copy-start | bytes 4718596
  235.6 6.1 copy-start.17
  249.3 7.9 %copy-start.19 = (f32[1,4,192,512]{3,2,0,1:T(8,128)S(1)}, f32[1,4,192,512]{3,2,0,1:T(8,128)}, u32[]{:S(2)}) copy-start(f32[1,4,192,512]{3,2,0,1:T(8,128)} %get-tuple-element.46) | copy-start | bytes 4718596
  249.3 7.9 %copy-start.25 = (bf16[768,512]{1,0:T(8,128)(2,1)S(1)}, bf16[768,512]{1,0:T(8,128)(2,1)}, u32[]{:S(2)}) copy-start(bf16[768,512]{1,0:T(8,128)(2,1)} %copy.135) | copy-start | bytes 2359300
  249.3 16.8 %slice-start.2 = ((s8[12582912]{0:T(1024)(128)(4,1)}), s8[4194304]{0:T(1024)(128)(4,1)S(1)}, s32[]{:S(2)}) async-start(s8[12582912]{0:T(1024)(128)(4,1)} %bitcast.297), calls=%async_computation.24 | async-start | bytes 8388608
  249.3 16.8 %slice-start.3 = ((s8[12582912]{0:T(1024)(128)(4,1)}), s8[4194304]{0:T(1024)(128)(4,1)S(1)}, s32[]{:S(2)}) async-start(s8[12582912]{0:T(1024)(128)(4,1)} %bitcast.297), calls=%async_computation.25 | async-start | bytes 8388608
  257.2 8.9 %slice-start.4 = ((s8[12582912]{0:T(1024)(128)(4,1)}), s8[4194304]{0:T(1024)(128)(4,1)S(1)}, s32[]{:S(2)}) async-start(s8[12582912]{0:T(1024)(128)(4,1)} %bitcast.297), calls=%async_computation.26 | async-start | bytes 8388608
  266.1 6.4 %copy-start.15 = (f32[1,4,192,512]{3,2,0,1:T(8,128)S(1)}, f32[1,4,192,512]{3,2,0,1:T(8,128)}, u32[]{:S(2)}) copy-start(f32[1,4,192,512]{3,2,0,1:T(8,128)} %get-tuple-element.45) | copy-start | bytes 4718596
  279.3 103.8 %reduce-scatter.5.cloned.1.call-start = ((), (), s32[]{:S(2)}) async-start(), calls=%async_computation.12 | async-start | bytes 4091904 | tf_op jit(solution)/shard_map/reduce_scatter | solution.py:201
  298.7 142.2 %reduce-scatter.11.cloned.1.call-start = ((), (), s32[]{:S(2)}) async-start(), calls=%async_computation.15 | async-start | bytes 5308416 | tf_op jit(solution)/shard_map/reduce_scatter | solution.py:201
  312.0 186.2 %reduce-scatter.9.cloned.1.call-start = ((), (), s32[]{:S(2)}) async-start(), calls=%async_computation.14 | async-start | bytes 5308416 | tf_op jit(solution)/shard_map/reduce_scatter | solution.py:201
  361.8 137.9 %all-to-all-start.2 = ((bf16[8,96,512]{2,1,0:T(8,128)(2,1)}), bf16[8,96,512]{2,1,0:T(8,128)(2,1)S(1)}, u32[]{:S(2)}, u32[]{:S(2)}) async-start(bf16[8,96,512]{2,1,0:T(8,128)(2,1)} %get-tuple-element.48), calls=%async_computation.2 | async-start | bytes 1572864 | tf_op jit(solution)/shard_map/all_to_all | solution.py:90
  365.4 226.4 %all-reduce.8.cloned.1.call-start = ((), (), s32[]{:S(2)}) async-start(), calls=%async_computation.21 | async-start | bytes 3563520 | tf_op jit(solution)/shard_map/psum | solution.py:201
  499.7 31.5 %all-to-all-start.7 = ((bf16[2,8,96,256]{3,1,2,0:T(8,128)(2,1)}), bf16[2,8,96,256]{3,1,2,0:T(8,128)(2,1)S(1)}, u32[]{:S(2)}, u32[]{:S(2)}) async-start(bf16[2,8,96,256]{3,1,2,0:T(8,128)(2,1)} %copy.140), calls=%async_computation.7 | async-start | bytes 1572864 | tf_op jit(solution)/shard_map/all_to_all | solution.py:92
  531.3 20.7 %all-to-all-start.3 = ((bf16[2,8,96,256]{3,1,2,0:T(8,128)(2,1)}), bf16[2,8,96,256]{3,1,2,0:T(8,128)(2,1)S(1)}, u32[]{:S(2)}, u32[]{:S(2)}) async-start(bf16[2,8,96,256]{3,1,2,0:T(8,128)(2,1)} %copy.128), calls=%async_computation.3 | async-start | bytes 1572864 | tf_op jit(solution)/shard_map/all_to_all | solution.py:92
  (40 other events, 109.5 us)
Sparse Core Ops, SparseCore 0:
  12.1 54.8 all-reduce.5
  69.1 42.3 all-gather.9
  113.5 24.0 all-gather.11
  139.5 38.9 all-gather.13
  180.4 38.9 all-gather.15
  279.4 36.7 reduce-scatter.6
  319.7 63.2 reduce-scatter.4
  386.9 53.9 reduce-scatter.10
  444.3 53.8 reduce-scatter.8
  500.9 90.8 all-reduce.7

commit v2 on v1

--- a/solution.py
+++ b/solution.py
@@ -92,14 +92,29 @@
         v = lax.all_to_all(v, "dp", 0, 0, axis_index_groups=groups, tiled=True)
         return jnp.transpose(v, (2, 0, 1, 3)).reshape(tokens.shape)
 
+    def flip_row(v):
+        return lax.ppermute(v, "row", [(i, i ^ 1) for i in range(nr)])
+
+    def flip_chip(v):
+        return lax.ppermute(v, "col", [(i, i ^ 2) for i in range(nc)])
+
+    def flip_core(v):
+        return lax.ppermute(v, "col", [(i, i ^ 1) for i in range(nc)])
+
     def gather(v):
-        return lax.all_gather(v, RC, axis=0)
-
-    ga = gather(attend_weight)
-    go = gather(output_weight)
+        h = v.shape[0] // 2
+        by_row, by_chip = flip_row(v), flip_chip(v)
+        far0, far1 = flip_row(by_chip[:h]), flip_chip(by_row[h:])
+        own = [v, by_chip, by_row, far0, far1]
+        other = [flip_core(p) for p in own]
+        v1, c1, r1, f1, g1 = other
+        return jnp.concatenate([v, v1, by_chip, c1, by_row, r1, far0, far1, f1, g1], axis=0).reshape((n,) + v.shape)
+
+    hw, rw, fw = output_weight.shape[0], output_weight.shape[1], shrink_weight.shape[0]
+    gao = gather(jnp.concatenate([attend_weight.reshape(3 * hw, rw), output_weight], axis=0))
+    ga, go = gao[:, : 3 * hw], gao[:, 3 * hw :]
     ge = gather(expand_weight)
     gs = gather(shrink_weight)
-    hw, rw, fw = output_weight.shape[0], output_weight.shape[1], shrink_weight.shape[0]
 
     thin = jnp.concatenate(
         [
@@ -110,11 +125,14 @@
             )
         ]
     )
-    thin = lax.all_gather(thin, RC, axis=0)
+    thin = thin[None]
+    for flip in (flip_core, flip_chip, flip_row):
+        thin = jnp.concatenate([thin, flip(thin)], axis=0)
+    flat_order = jnp.arange(n) ^ rc
     sizes = [fl] * 6 + [hw] * 4 + [fw] * 3
     cols, at = [], 0
     for i, size in enumerate(sizes):
-        piece = thin[:, at : at + size] if i < 6 else thin[:nc, at : at + size]
+        piece = thin[flat_order, at : at + size] if i < 6 else thin[:nc, at : at + size]
         cols.append(piece.reshape(-1, 1))
         at += size
     in_g, in_s, out_b, mid_g, mid_s, shr_b, q_b, v_b, mix_g, mix_s, exp_b, hid_g, hid_s = cols
@@ -132,8 +150,18 @@
 
     a, vh_in, r_in = norm(x, in_g, in_s)
     a = a.astype(bf16)
+    my_row = lax.axis_index("row")
+
+    def by_row_rel(v):
+        v = v.reshape(nr, rw, unit)
+        return jnp.where(my_row == 0, v, v[::-1])
+
+    def by_row_abs(v):
+        return jnp.where(my_row == 0, v, v[::-1]).reshape(nr * rw, unit)
+
+    a_rel = by_row_rel(a)
     gar = ga.reshape(nr, nc, 3, hw, rw)
-    trip = mm("rcjif,rft->jcit", gar, a.reshape(nr, rw, unit)).reshape(3, nc * hw, unit)
+    trip = mm("rcjif,rft->jcit", gar, a_rel).reshape(3, nc * hw, unit)
     heads = lambda v: v.reshape(-1, HEAD, unit)
     q = heads((trip[0] + q_b).astype(bf16))
     k = heads(trip[1].astype(bf16))
@@ -147,20 +175,21 @@
     on, vh_mix, r_mix = norm(o, mix_g, mix_s)
     on = on.astype(bf16)
     gor = go.reshape(nr, nc * hw, rw)
-    x1 = x + mm("rin,it->rnt", gor, on).reshape(nr * rw, unit) + out_b
+    x1 = x + by_row_abs(mm("rin,it->rnt", gor, on)) + out_b
     b, vh_mid, r_mid = norm(x1, mid_g, mid_s)
     b = b.astype(bf16)
     ger = ge.reshape(nr, nc, rw, fw)
-    f = mm("rckn,rkt->cnt", ger, b.reshape(nr, rw, unit)).reshape(nc * fw, unit) + exp_b
+    b_rel = by_row_rel(b)
+    f = mm("rckn,rkt->cnt", ger, b_rel).reshape(nc * fw, unit) + exp_b
     phi = 0.5 * (1.0 + lax.erf(f * math.sqrt(0.5)))
     g = f * phi
     gn, vh_hid, r_hid = norm(g, hid_g, hid_s)
     gn = gn.astype(bf16)
     gsr = gs.reshape(nr, nc * fw, rw)
-    y = x1 + mm("rfn,ft->rnt", gsr, gn).reshape(nr * rw, unit) + shr_b
+    y = x1 + by_row_abs(mm("rfn,ft->rnt", gsr, gn)) + shr_b
     block_out = from_unit(y.astype(bf16))
 
-    e2r = e2.reshape(nr, rw, unit)
+    e2r = by_row_rel(e2)
     d_shr_w = mm("cft,rdt->rcfd", gn.reshape(nc, fw, unit), e2r).astype(bf16)
     dy = e2.astype(f32)
     d_shr_b = jnp.sum(dy, axis=1, keepdims=True)
@@ -170,13 +199,13 @@
     df = (dg * slope).astype(bf16)
     d_exp_b = jnp.sum(df.astype(f32), axis=1, keepdims=True)
     dfc = df.reshape(nc, fw, unit)
-    d_exp_w = mm("rkt,cnt->rckn", b.reshape(nr, rw, unit), dfc).astype(bf16)
-    db = mm("rckn,cnt->rkt", ger, dfc).reshape(nr * rw, unit)
+    d_exp_w = mm("rkt,cnt->rckn", b_rel, dfc).astype(bf16)
+    db = by_row_abs(mm("rckn,cnt->rkt", ger, dfc))
     dx1, d_mid_g, d_mid_s = norm_back(db, vh_mid, r_mid, mid_g)
     dx1 = dy + dx1
     e1 = dx1.astype(bf16)
     d_out_b = jnp.sum(e1.astype(f32), axis=1, keepdims=True)
-    e1r = e1.reshape(nr, rw, unit)
+    e1r = by_row_rel(e1)
     d_out_w = mm("cit,rnt->rcin", on.reshape(nc, hw, unit), e1r).astype(bf16)
     don = mm("rin,rnt->it", gor, e1r)
     do, d_mix_g, d_mix_s = norm_back(don, vh_mix, r_mix, mix_g)
@@ -191,32 +220,44 @@
     d_q_b = jnp.sum(dq.astype(f32), axis=2)
     d_v_b = jnp.sum(dv.astype(f32), axis=2)
     dtrip = jnp.stack([dq, dk, dv], axis=1)
-    d_att_w = mm("cjit,rft->rcjif", dtrip, a.reshape(nr, rw, unit)).astype(bf16)
-    da = mm("rcjif,cjit->rft", gar, dtrip).reshape(nr * rw, unit)
+    d_att_w = mm("cjit,rft->rcjif", dtrip, a_rel).astype(bf16)
+    da = by_row_abs(mm("rcjif,cjit->rft", gar, dtrip))
     dx, d_in_g, d_in_s = norm_back(da, vh_in, r_in, in_g)
     input_grad = from_unit((dx1 + dx).astype(bf16))
 
     def reduce(v):
-        v = v.reshape((n,) + v.shape[2:])
-        return lax.psum(lax.psum_scatter(v, RC, scatter_dimension=0, tiled=False), "dp")
+        v = v.reshape((nr, nc // 2, 2) + v.shape[2:])
+        v = v[:, :, 0] + flip_core(v[:, :, 1])
+        h = v.shape[2] // 2
+        p, q = v[:, :, :h], v[:, :, h:]
+        p = p[0] + flip_row(p[1])
+        q = q[:, 0] + flip_chip(q[:, 1])
+        p = p[0] + flip_chip(p[1])
+        q = q[0] + flip_row(q[1])
+        v = jnp.concatenate([p, q], axis=0)
+        step = 1
+        while step < holders:
+            v = v + lax.ppermute(v, "dp", [(i, i ^ step) for i in range(holders)])
+            step *= 2
+        return v
 
     shr_w_g = reduce(d_shr_w).astype(f32)
     exp_w_g = reduce(d_exp_w).astype(f32)
-    out_w_g = reduce(d_out_w).astype(f32)
-
-    by_rc = [v.reshape(n, fl) for v in (d_in_g, d_in_s, d_out_b, d_mid_g, d_mid_s, d_shr_b)]
+
+    by_rc = [v.reshape(n, fl)[flat_order] for v in (d_in_g, d_in_s, d_out_b, d_mid_g, d_mid_s, d_shr_b)]
     by_c = [
         jnp.broadcast_to(v.reshape(1, nc, -1), (nr, nc, v.size // nc)).reshape(n, -1)
         for v in (d_q_b, d_v_b, d_mix_g, d_mix_s, d_exp_b, d_hid_g, d_hid_s)
     ]
     small = jnp.concatenate(by_rc + by_c, axis=1).astype(bf16)
     width = small.shape[1]
-    pad = -width % rw
+    pad = -width % (2 * rw)
     small = jnp.pad(small, ((0, 0), (0, pad))).reshape(nr, nc, -1, rw)
-    last = jnp.concatenate([d_att_w.reshape(nr, nc, 3 * hw, rw), small], axis=2)
+    last = jnp.concatenate([d_att_w.reshape(nr, nc, 3 * hw, rw), d_out_w, small], axis=2)
     last = reduce(last).astype(f32)
+    out_w_g = last[3 * hw : 4 * hw]
     att_w_g = last[: 3 * hw].reshape(attend_weight.shape)
-    flat = last[3 * hw :].reshape(-1)
+    flat = last[4 * hw :].reshape(-1)
     outs, at = [], 0
     for size in sizes:
         outs.append(flat[at : at + size])

time: 613 us -> 559 us (0.912)
  waiting for transfers between devices: 337 us -> 117 us
  local copies, waits for them, and re-layouts: 60.3 us -> 227 us
  starting transfers between devices: 27.1 us -> 77.3 us
  matrix products: 99.4 us -> 67.3 us
  blocking collectives: 20.6 us -> 0 us
  between operations: 18.1 us -> 4.39 us
  other arithmetic: 44.9 us -> 54.5 us
    reduce_scatter x4 -> x0, waiting for transfers between devices: 133 us -> none  [reduce(): lax.psum_scatter(v, RC, scatter_dimension=0, tiled=False)]
    ppermute x0 -> x51, waiting for transfers between devices: none -> 101 us  [the longest x6 66.2 us: reduce(): v = v + lax.ppermute(v, 'dp', [(i, i ^ step) for i in range(holders)])]
    gather x0 -> x198, local copies, waits for them, and re-layouts: none -> 98.9 us
    all_gather x4 -> x0, waiting for transfers between devices: 88.1 us -> none  [gather(): return lax.all_gather(v, RC, axis=0)]
    unnamed x117 -> x210, local copies, waits for them, and re-layouts: 11.9 us -> 63.7 us
    ppermute x0 -> x51, starting transfers between devices: none -> 47.4 us  [the longest x13 18 us: flip_row(): return lax.ppermute(v, 'row', [(i, i ^ 1) for i in range(nr)])]
    psum x1 -> x0, waiting for transfers between devices: 38.5 us -> none  [reduce(): lax.psum(lax.psum_scatter(v, RC, scatter_dimension=0, tiled=False), 'dp')]
    dot_general x17, matrix products: 88.7 us -> 56.5 us  [mm(): return jnp.einsum(spec, a, b, preferred_element_type=f32)]
  transfers between devices with their start and end apart: 17 -> 59, of which waited for: 12 -> 20; matrix products, arithmetic and copies ran while one was open for 21% -> 45% of each run, Pallas kernels for 0% -> 0%
where the time goes in v2:
time: 559 us; the launch traced here: 548 us
  local copies, waits for them, and re-layouts  227 us (41%)
  waiting for transfers between devices  117 us (21%)
  starting transfers between devices  77.3 us (14%)
  matrix products  67.3 us (12%)
  other arithmetic  54.5 us (10%)
    gather x192, local copies, waits for them, and re-layouts  95.5 us
    ppermute x6, waiting for transfers between devices, reduce(): v = v + lax.ppermute(v, 'dp', [(i, i ^ step) for i in range(holders)])  66.2 us
    unnamed x210, local copies, waits for them, and re-layouts  63.7 us
    dot_general x17, matrix products, mm(): return jnp.einsum(spec, a, b, preferred_element_type=f32)  56.5 us
    ppermute x13, waiting for transfers between devices, flip_row(): return lax.ppermute(v, 'row', [(i, i ^ 1) for i in range(nr)])  28.8 us
    ppermute x13, starting transfers between devices, flip_row(): return lax.ppermute(v, 'row', [(i, i ^ 1) for i in range(nr)])  18 us
    ppermute x13, starting transfers between devices, flip_chip(): return lax.ppermute(v, 'col', [(i, i ^ 2) for i in range(nc)])  16.4 us
    all_to_all x2, waiting for transfers between devices, from_unit(): v = lax.all_to_all(v, 'dp', 0, 0, axis_index_groups=groups, tiled=True)  12.2 us
  transfers between devices with their start and end apart: 59, of which 20 were waited for; matrix products, arithmetic and copies ran while one was open for 45% of the time, Pallas kernels for 0%

profile of v2, /device:TPU:0, one launch (start us, length us, event | category | flops | bytes accessed | tf_op | source)
XLA Modules:
  0.0 548.1 jit_solution(16052869131844431311)
XLA Ops:
  29.3 4.6 collective-permute-done.10
  40.8 16.0 %while.11 = (s32[]{:T(128)}, f32[8,3648]{1,0:T(8,128)S(1)}, s32[8,2]{0,1:T(2,128)S(1)}, f32[8,96]{1,0:T(8,128)S(1)}, s32[]{:T(128)}, /*index=5*/s32[]{:T(128)}) while((s32[]{:T(128)}, f32[8,3648]{1,0:T(8,128)S(1)}, s32[8,2]{0,1:T(2,128)S(1)}, f32[8,96]{1,0:T(8,128)S(1)}, s32[]{:T(128)}, /*index=5*/s32[]{:T(128)}) %tuple.164), condition=%wide.while_cond.5, body=%wide.while_body.5.sunk | while | flops 2 | bytes 1657 | solution.py:135
  56.8 16.0 %while.10 = (s32[]{:T(128)}, f32[8,3648]{1,0:T(8,128)S(1)}, s32[8,2]{0,1:T(2,128)S(1)}, f32[8,96]{1,0:T(8,128)S(1)}, s32[]{:T(128)}, /*index=5*/s32[]{:T(128)}) while((s32[]{:T(128)}, f32[8,3648]{1,0:T(8,128)S(1)}, s32[8,2]{0,1:T(2,128)S(1)}, f32[8,96]{1,0:T(8,128)S(1)}, s32[]{:T(128)}, /*index=5*/s32[]{:T(128)}) %tuple.167), condition=%wide.while_cond.4, body=%wide.while_body.4.sunk | while | flops 2 | bytes 1657 | solution.py:135
  72.8 16.0 %while.9 = (s32[]{:T(128)}, f32[8,3648]{1,0:T(8,128)S(1)}, s32[8,2]{0,1:T(2,128)S(1)}, f32[8,96]{1,0:T(8,128)S(1)}, s32[]{:T(128)}, /*index=5*/s32[]{:T(128)}) while((s32[]{:T(128)}, f32[8,3648]{1,0:T(8,128)S(1)}, s32[8,2]{0,1:T(2,128)S(1)}, f32[8,96]{1,0:T(8,128)S(1)}, s32[]{:T(128)}, /*index=5*/s32[]{:T(128)}) %tuple.168), condition=%wide.while_cond.3, body=%wide.while_body.3.sunk | while | flops 2 | bytes 1657 | solution.py:135
  88.8 16.0 %while.8 = (s32[]{:T(128)}, f32[8,3648]{1,0:T(8,128)S(1)}, s32[8,2]{0,1:T(2,128)S(1)}, f32[8,96]{1,0:T(8,128)S(1)}, s32[]{:T(128)}, /*index=5*/s32[]{:T(128)}) while((s32[]{:T(128)}, f32[8,3648]{1,0:T(8,128)S(1)}, s32[8,2]{0,1:T(2,128)S(1)}, f32[8,96]{1,0:T(8,128)S(1)}, s32[]{:T(128)}, /*index=5*/s32[]{:T(128)}) %tuple.169), condition=%wide.while_cond.2, body=%wide.while_body.2.sunk | while | flops 2 | bytes 1657 | solution.py:135
  104.8 16.0 %while.7 = (s32[]{:T(128)}, f32[8,3648]{1,0:T(8,128)S(1)}, s32[8,2]{0,1:T(2,128)S(1)}, f32[8,96]{1,0:T(8,128)S(1)}, s32[]{:T(128)}, /*index=5*/s32[]{:T(128)}) while((s32[]{:T(128)}, f32[8,3648]{1,0:T(8,128)S(1)}, s32[8,2]{0,1:T(2,128)S(1)}, f32[8,96]{1,0:T(8,128)S(1)}, s32[]{:T(128)}, /*index=5*/s32[]{:T(128)}) %tuple.170), condition=%wide.while_cond.1, body=%wide.while_body.1.sunk | while | flops 2 | bytes 1657 | solution.py:135
  126.7 16.0 %while.6 = (s32[]{:T(128)}, f32[8,3648]{1,0:T(8,128)S(1)}, s32[8,2]{0,1:T(2,128)S(1)}, f32[8,96]{1,0:T(8,128)S(1)}, s32[]{:T(128)}, /*index=5*/s32[]{:T(128)}) while((s32[]{:T(128)}, f32[8,3648]{1,0:T(8,128)S(1)}, s32[8,2]{0,1:T(2,128)S(1)}, f32[8,96]{1,0:T(8,128)S(1)}, s32[]{:T(128)}, /*index=5*/s32[]{:T(128)}) %tuple.171), condition=%wide.while_cond, body=%wide.while_body.sunk | while | flops 2 | bytes 1657 | solution.py:135
  166.4 3.9 all-to-all-start.1
  207.8 4.2 slice.358
  212.0 6.7 %copy.135 = bf16[4,768,384,2]{2,1,0,3:T(8,128)(2,1)} copy(bf16[4,768,384,2]{1,2,0,3:T(8,128)(2,1)} %bitcast.392) | data formatting | bytes 9437184 | tf_op jit(solution)/shard_map/rckn,rkt->cnt/dot_general | solution.py:17
  221.0 4.0 all-to-all-start.5
  232.3 4.2 all-to-all-done.5
  237.6 10.8 %fusion.88 = (f32[12,512]{1,0:T(8,128)S(1)}, f32[12,512,512]{2,1,0:T(8,128)}) fusion(pred[512,512]{1,0:T(8,128)(4,1)S(1)} %copy-done.51, bf16[12,64,512]{2,1,0:T(8,128)(2,1)S(1)} %bitcast.385, f32[12,64,512]{2,1,0:T(8,128)} %bitcast.387, f32[12,64]{1,0:T(8,128)S(1)} %copy-done.64), kind=kOutput, calls=%fused_computation.252 | convolution fusion | flops 416023040 | bytes 15232000 | tf_op jit(solution)/shard_map/sub | solution.py:171
  248.4 6.4 %fusion.89 = (f32[512]{0:T(512)S(1)}, f32[12,64,512]{2,1,0:T(8,128)S(1)}) fusion(f32[12,512,512]{2,1,0:T(8,128)} %get-tuple-element.193, f32[12,512]{1,0:T(8,128)S(1)} %get-tuple-element.192, f32[12,64,512]{2,1,0:T(8,128)} %bitcast.425, f32[12,64]{1,0:T(8,128)S(1)} %copy-done.74), kind=kOutput, calls=%fused_computation.253 | convolution fusion | flops 410123776 | bytes 15758336 | tf_op jit(solution)/shard_map/hek,hkq->heq/dot_general | solution.py:17
  259.4 3.8 fusion.70
  264.3 6.8 %fusion.8 = (bf16[3072]{0:T(1024)(128)(2,1)S(1)}, f32[512]{0:T(512)S(1)}, f32[512]{0:T(512)S(1)}, bf16[3072]{0:T(1024)(128)(2,1)S(1)}, bf16[3072,512]{1,0:T(8,128)(2,1)S(1)}, /*index=5*/f32[3072,512,1]{1,0,2:T(8,128)S(1)}) fusion(f32[3072,512]{1,0:T(8,128)S(1)} %get-tuple-element.137, f32[512]{0:T(512)S(1)} %add_rsqrt_fusion, ...), kind=kOutput, calls=%fused_computation.28 | convolution fusion | flops 2434786304 | bytes 21278720 | tf_op jit(solution)/shard_map/rfd,rdt->ft/dot_general | solution.py:17
  271.2 5.7 %fusion.14 = f32[2,384,512]{2,1,0:T(8,128)S(1)} fusion(bf16[2,3072,384]{2,1,0:T(8,128)(2,1)} %bitcast.21, bf16[3072,512]{1,0:T(8,128)(2,1)S(1)} %get-tuple-element.153), kind=kOutput, calls=%fused_computation.42 | convolution fusion | flops 2415919104 | bytes 9437184 | tf_op jit(solution)/shard_map/rfn,ft->rnt/dot_general | solution.py:17
  276.9 6.9 %fusion.68 = (bf16[3072]{0:T(1024)(128)(2,1)S(1)}, bf16[3072,512]{1,0:T(8,128)(2,1)S(1)}) fusion(f32[3072]{0:T(1024)S(1)} %copy-done.55, f32[3072,512,1]{1,0,2:T(8,128)S(1)} %get-tuple-element.196, f32[512]{0:T(512)S(1)} %broadcast_multiply_fusion, f32[3072,512]{1,0:T(8,128)S(1)} %get-tuple-element.137, f32[512]{0:T(512)S(1)} %broadcast_multiply_fusion.2, ...), kind=kLoop, calls=%fused_computation.235 | loop fusion | flops 29881344 | bytes 22059008 | tf_op jit(solution)/shard_map/reduce_sum | solution.py:200
  297.3 5.9 %multiply_reduce_fusion = (f32[12,512]{1,0:T(8,128)S(1)}, f32[12,512,512]{2,1,0:T(8,128)}) fusion(f32[12,512,512]{2,1,0:T(8,128)S(1)} %bitcast.384, f32[12,512]{1,0:T(8,128)S(1)} %get-tuple-element.192, bf16[12,64,512]{2,1,0:T(8,128)(2,1)S(1)} %bitcast.438, f32[12,64,512]{2,1,0:T(8,128)S(1)} %bitcast.426, f32[12,64]{1,0:T(8,128)S(1)} %copy-done.74), kind=kOutput, calls=%fused_computation.14 | convolution fusion | flops 412870656 | bytes 27577344 | tf_op jit(solution)/shard_map/hek,heq->hkq/dot_general | solution.py:17
  303.2 7.2 %multiply_convert_fusion = bf16[12,512,512]{2,1,0:T(8,128)(2,1)S(1)} fusion(f32[12,512,512]{2,1,0:T(8,128)} %get-tuple-element.200, f32[12,512]{1,0:T(8,128)S(1)} %get-tuple-element.199, f32[12,512,512]{2,1,0:T(8,128)S(1)} %bitcast.384, f32[12,512]{1,0:T(8,128)S(1)} %get-tuple-element.192), kind=kLoop, calls=%fused_computation.13 | loop fusion | flops 12582912 | bytes 31506432 | tf_op jit(solution)/shard_map/convert_element_type | solution.py:215
  328.1 4.3 copy.180
  332.4 4.8 fusion.33
  365.8 3.9 all-to-all-start.2
  390.1 4.3 collective-permute-done.38
  397.7 9.3 %collective-permute-done.45 = bf16[2,384,384]{2,1,0:T(8,128)(2,1)S(1)} collective-permute-done((bf16[2,384,384]{2,1,0:T(8,128)(2,1)S(1)}, bf16[2,384,384]{2,1,0:T(8,128)(2,1)S(1)}, u32[]{:S(2)}, u32[]{:S(2)}) %collective-permute-start.45) | collective-permute-done | bytes 589856 | tf_op jit(solution)/shard_map/ppermute | solution.py:96
  411.1 8.8 %collective-permute-done.31 = bf16[2,389,384]{2,0,1:T(2,128)(2,1)S(1)} collective-permute-done((bf16[2,389,384]{2,0,1:T(2,128)(2,1)S(1)}, bf16[2,389,384]{2,0,1:T(2,128)(2,1)S(1)}, u32[]{:S(2)}, u32[]{:S(2)}) %collective-permute-start.31) | collective-permute-done | bytes 597536 | tf_op jit(solution)/shard_map/ppermute | solution.py:96
  432.6 3.8 all-to-all-start.7
  445.1 8.6 %all-to-all-done.7 = bf16[2,8,96,256]{3,1,2,0:T(8,128)(2,1)S(1)} async-done(((bf16[2,8,96,256]{3,1,2,0:T(8,128)(2,1)}), bf16[2,8,96,256]{3,1,2,0:T(8,128)(2,1)S(1)}, u32[]{:S(2)}, u32[]{:S(2)}) %all-to-all-start.7) | async-done | bytes 786464 | tf_op jit(solution)/shard_map/all_to_all | solution.py:92
  462.0 17.1 %collective-permute-done.49 = bf16[768,384]{1,0:T(8,128)(2,1)} collective-permute-done((bf16[768,384]{1,0:T(8,128)(2,1)}, bf16[768,384]{1,0:T(8,128)(2,1)}, u32[]{:S(2)}, u32[]{:S(2)}) %collective-permute-start.49) | collective-permute-done | bytes 589856 | tf_op jit(solution)/shard_map/ppermute | solution.py:240
  482.6 17.4 %collective-permute-done.35 = bf16[778,384]{1,0:T(8,128)(2,1)} collective-permute-done((bf16[778,384]{1,0:T(8,128)(2,1)}, bf16[778,384]{1,0:T(8,128)(2,1)}, u32[]{:S(2)}, u32[]{:S(2)}) %collective-permute-start.35) | collective-permute-done | bytes 597536 | tf_op jit(solution)/shard_map/ppermute | solution.py:240
  509.7 25.8 %collective-permute-done.50 = bf16[768,384]{1,0:T(8,128)(2,1)} collective-permute-done((bf16[768,384]{1,0:T(8,128)(2,1)S(1)}, bf16[768,384]{1,0:T(8,128)(2,1)}, u32[]{:S(2)}, u32[]{:S(2)}) %collective-permute-start.50) | collective-permute-done | bytes 589856 | tf_op jit(solution)/shard_map/ppermute | solution.py:240
  537.7 5.9 %collective-permute-done.36 = bf16[778,384]{1,0:T(8,128)(2,1)S(1)} collective-permute-done((bf16[778,384]{1,0:T(8,128)(2,1)S(1)}, bf16[778,384]{1,0:T(8,128)(2,1)S(1)}, u32[]{:S(2)}, u32[]{:S(2)}) %collective-permute-start.36) | collective-permute-done | bytes 597536 | tf_op jit(solution)/shard_map/ppermute | solution.py:240
  (694 shorter events, 348.5 us)
Async XLA Ops:
  2.6 118.1 %collective-permute-start.3 = (bf16[768,384]{1,0:T(8,128)(2,1)}, bf16[768,384]{1,0:T(8,128)(2,1)S(1)}, u32[]{:S(2)}, u32[]{:S(2)}) collective-permute-start(bf16[768,384]{1,0:T(8,128)(2,1)} %pad_maximum_fusion.5), channel_id=1, source_target_pairs={{0,4},{4,0},{1,5},{5,1},{2,6},{6,2},{3,7},{7,3},{8,12},{12,8},{9,1... | collective-permute-start | bytes 1769480 | tf_op jit(solution)/shard_map/ppermute | solution.py:96
  5.6 115.2 %collective-permute-start.1 = (bf16[768,384]{1,0:T(8,128)(2,1)}, bf16[768,384]{1,0:T(8,128)(2,1)S(1)}, u32[]{:S(2)}, u32[]{:S(2)}) collective-permute-start(bf16[768,384]{1,0:T(8,128)(2,1)} %pad_maximum_fusion.5), channel_id=1, source_target_pairs={{0,2},{1,3},{2,0},{3,1},{4,6},{5,7},{6,4},{7,5},{8,10},{9,11},{10,... | collective-permute-start | bytes 1769480 | tf_op jit(solution)/shard_map/ppermute | solution.py:99
  7.1 145.5 %collective-permute-start = (bf16[768,384]{1,0:T(8,128)(2,1)}, bf16[768,384]{1,0:T(8,128)(2,1)}, u32[]{:S(2)}, u32[]{:S(2)}) collective-permute-start(bf16[768,384]{1,0:T(8,128)(2,1)} %pad_maximum_fusion.5), channel_id=1, source_target_pairs={{0,1},{1,0},{2,3},{3,2},{4,5},{5,4},{6,7},{7,6},{8,9},{9,8},{10,11... | collective-permute-start | bytes 1769480 | tf_op jit(solution)/shard_map/ppermute | solution.py:102
  9.4 113.0 %collective-permute-start.22 = (bf16[384,768]{1,0:T(8,128)(2,1)}, bf16[384,768]{1,0:T(8,128)(2,1)}, u32[]{:S(2)}, u32[]{:S(2)}) collective-permute-start(bf16[384,768]{1,0:T(8,128)(2,1)} %param.34), channel_id=1, source_target_pairs={{0,2},{1,3},{2,0},{3,1},{4,6},{5,7},{6,4},{7,5},{8,10},{9,11},{10,... | collective-permute-start | bytes 1769480 | tf_op jit(solution)/shard_map/ppermute | solution.py:99
  12.2 110.9 %all-to-all-start = ((bf16[2,8,96,256]{3,1,2,0:T(8,128)(2,1)}), bf16[2,8,96,256]{3,1,2,0:T(8,128)(2,1)S(1)}, u32[]{:S(2)}, u32[]{:S(2)}) async-start(bf16[2,8,96,256]{3,1,2,0:T(8,128)(2,1)} %copy.131), calls=%async_computation | async-start | bytes 1572864 | tf_op jit(solution)/shard_map/all_to_all | solution.py:84
  39.0 83.5 %collective-permute-start.24 = (bf16[384,768]{1,0:T(8,128)(2,1)}, bf16[384,768]{1,0:T(8,128)(2,1)S(1)}, u32[]{:S(2)}, u32[]{:S(2)}) collective-permute-start(bf16[384,768]{1,0:T(8,128)(2,1)} %param.34), channel_id=1, source_target_pairs={{0,4},{4,0},{1,5},{5,1},{2,6},{6,2},{3,7},{7,3},{8,12},{12,8},{9,1... | collective-permute-start | bytes 1769480 | tf_op jit(solution)/shard_map/ppermute | solution.py:96
  120.7 35.2 %collective-permute-start.21 = (bf16[384,768]{1,0:T(8,128)(2,1)}, bf16[384,768]{1,0:T(8,128)(2,1)}, u32[]{:S(2)}, u32[]{:S(2)}) collective-permute-start(bf16[384,768]{1,0:T(8,128)(2,1)} %param.34), channel_id=1, source_target_pairs={{0,1},{1,0},{2,3},{3,2},{4,5},{5,4},{6,7},{7,6},{8,9},{9,8},{10,11... | collective-permute-start | bytes 1769480 | tf_op jit(solution)/shard_map/ppermute | solution.py:102
  120.8 27.9 %collective-permute-start.13 = (bf16[768,384]{1,0:T(8,128)(2,1)}, bf16[768,384]{1,0:T(8,128)(2,1)}, u32[]{:S(2)}, u32[]{:S(2)}) collective-permute-start(bf16[768,384]{1,0:T(8,128)(2,1)} %param.38), channel_id=1, source_target_pairs={{0,2},{1,3},{2,0},{3,1},{4,6},{5,7},{6,4},{7,5},{8,10},{9,11},{10,... | collective-permute-start | bytes 1769480 | tf_op jit(solution)/shard_map/ppermute | solution.py:99
  122.4 37.4 %collective-permute-start.12 = (bf16[768,384]{1,0:T(8,128)(2,1)}, bf16[768,384]{1,0:T(8,128)(2,1)}, u32[]{:S(2)}, u32[]{:S(2)}) collective-permute-start(bf16[768,384]{1,0:T(8,128)(2,1)} %param.38), channel_id=1, source_target_pairs={{0,1},{1,0},{2,3},{3,2},{4,5},{5,4},{6,7},{7,6},{8,9},{9,8},{10,11... | collective-permute-start | bytes 1769480 | tf_op jit(solution)/shard_map/ppermute | solution.py:102
  122.6 28.2 %collective-permute-start.15 = (bf16[768,384]{1,0:T(8,128)(2,1)}, bf16[768,384]{1,0:T(8,128)(2,1)}, u32[]{:S(2)}, u32[]{:S(2)}) collective-permute-start(bf16[768,384]{1,0:T(8,128)(2,1)} %param.38), channel_id=1, source_target_pairs={{0,4},{4,0},{1,5},{5,1},{2,6},{6,2},{3,7},{7,3},{8,12},{12,8},{9,1... | collective-permute-start | bytes 1769480 | tf_op jit(solution)/shard_map/ppermute | solution.py:96
  123.1 43.3 %all-to-all-start.4 = ((bf16[2,8,96,256]{3,1,2,0:T(8,128)(2,1)}), bf16[2,8,96,256]{3,1,2,0:T(8,128)(2,1)S(1)}, u32[]{:S(2)}, u32[]{:S(2)}) async-start(bf16[2,8,96,256]{3,1,2,0:T(8,128)(2,1)} %copy.139), calls=%async_computation.4 | async-start | bytes 1572864 | tf_op jit(solution)/shard_map/all_to_all | solution.py:84
  148.7 43.2 %collective-permute-start.6 = (bf16[384,384]{1,0:T(8,128)(2,1)}, bf16[384,384]{1,0:T(8,128)(2,1)}, u32[]{:S(2)}, u32[]{:S(2)}) collective-permute-start(bf16[384,384]{1,0:T(8,128)(2,1)} %slice.356), channel_id=1, source_target_pairs={{0,2},{1,3},{2,0},{3,1},{4,6},{5,7},{6,4},{7,5},{8,10},{9,11},{10,... | collective-permute-start | bytes 884744 | tf_op jit(solution)/shard_map/ppermute | solution.py:99
  150.8 33.9 %collective-permute-start.4 = (bf16[768,384]{1,0:T(8,128)(2,1)S(1)}, bf16[768,384]{1,0:T(8,128)(2,1)}, u32[]{:S(2)}, u32[]{:S(2)}) collective-permute-start(bf16[768,384]{1,0:T(8,128)(2,1)S(1)} %collective-permute-done.3), channel_id=1, source_target_pairs={{0,1},{1,0},{2,3},{3,2},{4,5},{5,4},{6,7},{7,6},{8,9},{9,8},{10,11... | collective-permute-start | bytes 1769480 | tf_op jit(solution)/shard_map/ppermute | solution.py:102
  166.4 54.6 %all-to-all-start.1 = ((bf16[8,96,512]{2,1,0:T(8,128)(2,1)}), bf16[8,96,512]{2,1,0:T(8,128)(2,1)S(1)}, u32[]{:S(2)}, u32[]{:S(2)}) async-start(bf16[8,96,512]{2,1,0:T(8,128)(2,1)} %reshape.717), calls=%async_computation.1 | async-start | bytes 1572864 | tf_op jit(solution)/shard_map/all_to_all | solution.py:86
  322.0 53.1 %collective-permute-start.37 = (bf16[2,2,384,768]{3,2,0,1:T(8,128)(2,1)}, bf16[2,2,384,768]{3,2,0,1:T(8,128)(2,1)}, u32[]{:S(2)}, u32[]{:S(2)}) collective-permute-start(bf16[2,2,384,768]{3,2,0,1:T(8,128)(2,1)} %slice_bitcast_fusion.2), channel_id=1, source_target_pairs={{0,1},{1,0},{2,3},{3,2},{4,5},{5,4},{6,7},{7,6},{8,9},{9,8},{10,11... | collective-permute-start | bytes 7077896 | tf_op jit(solution)/shard_map/ppermute | solution.py:102
  332.4 49.1 %collective-permute-start.44 = (bf16[2,2,768,384]{3,2,0,1:T(8,128)(2,1)}, bf16[2,2,768,384]{3,2,0,1:T(8,128)(2,1)}, u32[]{:S(2)}, u32[]{:S(2)}) collective-permute-start(bf16[2,2,768,384]{3,2,0,1:T(8,128)(2,1)} %bitcast.422), channel_id=1, source_target_pairs={{0,1},{1,0},{2,3},{3,2},{4,5},{5,4},{6,7},{7,6},{8,9},{9,8},{10,11... | collective-permute-start | bytes 7077896 | tf_op jit(solution)/shard_map/ppermute | solution.py:102
  361.5 23.1 %collective-permute-start.30 = (bf16[2,2,778,384]{3,1,2,0:T(2,128)(2,1)}, bf16[2,2,778,384]{3,1,2,0:T(2,128)(2,1)}, u32[]{:S(2)}, u32[]{:S(2)}) collective-permute-start(bf16[2,2,778,384]{3,1,2,0:T(2,128)(2,1)} %copy.150), channel_id=1, source_target_pairs={{0,1},{1,0},{2,3},{3,2},{4,5},{5,4},{6,7},{7,6},{8,9},{9,8},{10,11... | collective-permute-start | bytes 7170056 | tf_op jit(solution)/shard_map/ppermute | solution.py:102
  365.8 66.7 %all-to-all-start.2 = ((bf16[8,96,512]{2,1,0:T(8,128)(2,1)}), bf16[8,96,512]{2,1,0:T(8,128)(2,1)S(1)}, u32[]{:S(2)}, u32[]{:S(2)}) async-start(bf16[8,96,512]{2,1,0:T(8,128)(2,1)} %get-tuple-element.161), calls=%async_computation.2 | async-start | bytes 1572864 | tf_op jit(solution)/shard_map/all_to_all | solution.py:90
  383.5 23.5 %collective-permute-start.45 = (bf16[2,384,384]{2,1,0:T(8,128)(2,1)S(1)}, bf16[2,384,384]{2,1,0:T(8,128)(2,1)S(1)}, u32[]{:S(2)}, u32[]{:S(2)}) collective-permute-start(bf16[2,384,384]{2,1,0:T(8,128)(2,1)S(1)} %slice_bitcast_fusion.10), channel_id=1, source_target_pairs={{0,4},{4,0},{1,5},{5,1},{2,6},{6,2},{3,7},{7,3},{8,12},{12,8},{9,1... | collective-permute-start | bytes 1769480 | tf_op jit(solution)/shard_map/ppermute | solution.py:96
  384.2 24.6 %collective-permute-start.47 = (bf16[2,384,384]{2,1,0:T(8,128)(2,1)S(1)}, bf16[2,384,384]{2,1,0:T(8,128)(2,1)S(1)}, u32[]{:S(2)}, u32[]{:S(2)}) collective-permute-start(bf16[2,384,384]{2,1,0:T(8,128)(2,1)S(1)} %slice_bitcast_fusion.8), channel_id=1, source_target_pairs={{0,2},{1,3},{2,0},{3,1},{4,6},{5,7},{6,4},{7,5},{8,10},{9,11},{10,... | collective-permute-start | bytes 1769480 | tf_op jit(solution)/shard_map/ppermute | solution.py:99
  388.0 31.8 %collective-permute-start.31 = (bf16[2,389,384]{2,0,1:T(2,128)(2,1)S(1)}, bf16[2,389,384]{2,0,1:T(2,128)(2,1)S(1)}, u32[]{:S(2)}, u32[]{:S(2)}) collective-permute-start(bf16[2,389,384]{2,0,1:T(2,128)(2,1)S(1)} %copy.152), channel_id=1, source_target_pairs={{0,4},{4,0},{1,5},{5,1},{2,6},{6,2},{3,7},{7,3},{8,12},{12,8},{9,1... | collective-permute-start | bytes 1792520 | tf_op jit(solution)/shard_map/ppermute | solution.py:96
  394.4 27.2 %collective-permute-start.33 = (bf16[2,389,384]{2,0,1:T(2,128)(2,1)S(1)}, bf16[2,389,384]{2,0,1:T(2,128)(2,1)S(1)}, u32[]{:S(2)}, u32[]{:S(2)}) collective-permute-start(bf16[2,389,384]{2,0,1:T(2,128)(2,1)S(1)} %copy.154), channel_id=1, source_target_pairs={{0,2},{1,3},{2,0},{3,1},{4,6},{5,7},{6,4},{7,5},{8,10},{9,11},{10,... | collective-permute-start | bytes 1792520 | tf_op jit(solution)/shard_map/ppermute | solution.py:99
  396.3 29.9 %collective-permute-start.41 = (bf16[192,768]{1,0:T(8,128)(2,1)S(1)}, bf16[192,768]{1,0:T(8,128)(2,1)S(1)}, u32[]{:S(2)}, u32[]{:S(2)}) collective-permute-start(bf16[192,768]{1,0:T(8,128)(2,1)S(1)} %slice_bitcast_fusion.24), channel_id=1, source_target_pairs={{0,4},{4,0},{1,5},{5,1},{2,6},{6,2},{3,7},{7,3},{8,12},{12,8},{9,1... | collective-permute-start | bytes 884744 | tf_op jit(solution)/shard_map/ppermute | solution.py:96
  409.0 23.5 %collective-permute-start.48 = (bf16[384,384]{1,0:T(8,128)(2,1)S(1)}, bf16[384,384]{1,0:T(8,128)(2,1)S(1)}, u32[]{:S(2)}, u32[]{:S(2)}) collective-permute-start(bf16[384,384]{1,0:T(8,128)(2,1)S(1)} %slice_bitcast_fusion.20), channel_id=1, source_target_pairs={{0,4},{4,0},{1,5},{5,1},{2,6},{6,2},{3,7},{7,3},{8,12},{12,8},{9,1... | collective-permute-start | bytes 884744 | tf_op jit(solution)/shard_map/ppermute | solution.py:96
  428.9 28.4 %collective-permute-start.42 = (bf16[384,768]{1,0:T(8,128)(2,1)}, bf16[384,768]{1,0:T(8,128)(2,1)}, u32[]{:S(2)}, u32[]{:S(2)}) collective-permute-start(bf16[384,768]{1,0:T(8,128)(2,1)} %pad_maximum_fusion.6), channel_id=1, source_target_pairs={{0,8},{8,0},{16,24},{24,16},{1,9},{9,1},{17,25},{25,17},{2,10},{10... | collective-permute-start | bytes 1769480 | tf_op jit(solution)/shard_map/ppermute | solution.py:240
  432.6 21.2 %all-to-all-start.7 = ((bf16[2,8,96,256]{3,1,2,0:T(8,128)(2,1)}), bf16[2,8,96,256]{3,1,2,0:T(8,128)(2,1)S(1)}, u32[]{:S(2)}, u32[]{:S(2)}) async-start(bf16[2,8,96,256]{3,1,2,0:T(8,128)(2,1)} %copy.145), calls=%async_computation.7 | async-start | bytes 1572864 | tf_op jit(solution)/shard_map/all_to_all | solution.py:92
  438.4 40.8 %collective-permute-start.49 = (bf16[768,384]{1,0:T(8,128)(2,1)}, bf16[768,384]{1,0:T(8,128)(2,1)}, u32[]{:S(2)}, u32[]{:S(2)}) collective-permute-start(bf16[768,384]{1,0:T(8,128)(2,1)} %pad_maximum_fusion.7), channel_id=1, source_target_pairs={{0,8},{8,0},{16,24},{24,16},{1,9},{9,1},{17,25},{25,17},{2,10},{10... | collective-permute-start | bytes 1769480 | tf_op jit(solution)/shard_map/ppermute | solution.py:240
  443.4 56.6 %collective-permute-start.35 = (bf16[778,384]{1,0:T(8,128)(2,1)}, bf16[778,384]{1,0:T(8,128)(2,1)}, u32[]{:S(2)}, u32[]{:S(2)}) collective-permute-start(bf16[778,384]{1,0:T(8,128)(2,1)} %pad_maximum_fusion.4), channel_id=1, source_target_pairs={{0,8},{8,0},{16,24},{24,16},{1,9},{9,1},{17,25},{25,17},{2,10},{10... | collective-permute-start | bytes 1792520 | tf_op jit(solution)/shard_map/ppermute | solution.py:240
  453.8 52.4 %all-to-all-start.3 = ((bf16[2,8,96,256]{3,1,2,0:T(8,128)(2,1)}), bf16[2,8,96,256]{3,1,2,0:T(8,128)(2,1)S(1)}, u32[]{:S(2)}, u32[]{:S(2)}) async-start(bf16[2,8,96,256]{3,1,2,0:T(8,128)(2,1)} %copy.137), calls=%async_computation.3 | async-start | bytes 1572864 | tf_op jit(solution)/shard_map/all_to_all | solution.py:92
  459.4 47.9 %collective-permute-start.43 = (bf16[384,768]{1,0:T(8,128)(2,1)}, bf16[384,768]{1,0:T(8,128)(2,1)}, u32[]{:S(2)}, u32[]{:S(2)}) collective-permute-start(bf16[384,768]{1,0:T(8,128)(2,1)} %fusion.66), channel_id=1, source_target_pairs={{0,16},{8,24},{16,0},{24,8},{1,17},{9,25},{17,1},{25,9},{2,18},{10... | collective-permute-start | bytes 1769480 | tf_op jit(solution)/shard_map/ppermute | solution.py:240
  480.4 55.1 %collective-permute-start.50 = (bf16[768,384]{1,0:T(8,128)(2,1)S(1)}, bf16[768,384]{1,0:T(8,128)(2,1)}, u32[]{:S(2)}, u32[]{:S(2)}) collective-permute-start(bf16[768,384]{1,0:T(8,128)(2,1)S(1)} %fusion.65), channel_id=1, source_target_pairs={{0,16},{8,24},{16,0},{24,8},{1,17},{9,25},{17,1},{25,9},{2,18},{10... | collective-permute-start | bytes 1769480 | tf_op jit(solution)/shard_map/ppermute | solution.py:240
  501.2 42.4 %collective-permute-start.36 = (bf16[778,384]{1,0:T(8,128)(2,1)S(1)}, bf16[778,384]{1,0:T(8,128)(2,1)S(1)}, u32[]{:S(2)}, u32[]{:S(2)}) collective-permute-start(bf16[778,384]{1,0:T(8,128)(2,1)S(1)} %fusion.67), channel_id=1, source_target_pairs={{0,16},{8,24},{16,0},{24,8},{1,17},{9,25},{17,1},{25,9},{2,18},{10... | collective-permute-start | bytes 1792520 | tf_op jit(solution)/shard_map/ppermute | solution.py:240
  (112 other events, 1097.7 us)
